TPU v7x, 32 devices: a whole 2x2x4 slice. The times are simulated.
32 devices in a mesh: groups: 2 (over y), row: 4 (over z), col: 4 (over x, core).
Axes of the slice: x: 2, y: 2, z: 4, core: 2. Of those that a mesh axis runs over, the one named last changes fastest.
Arguments:
- queries: bfloat16 [4096, 1024], P(('groups', 'row'), 'col'), parts along dimension 0, may hold values from -64 to 64
- keys: bfloat16 [4096, 1024], P(('groups', 'col'), 'row'), parts along dimension 0, may hold values from -6 to 6
- values: bfloat16 [4096, 1024], P(('groups', 'col'), 'row'), parts along dimension 0, may hold values from -6 to 6
- cotangent: bfloat16 [4096, 1024], P(('groups', 'row'), 'col'), parts along dimension 0, may hold values from -6 to 6
- block_lists: int32 [32, 16], P(('groups', 'row')), parts along dimension 0, may hold values from 0 to 15, as said below
- block_counts: int32 [32], P(('groups', 'row')), parts along dimension 0, may hold values from 1 to 16, as said below
Outputs:
- attended: bfloat16 [4096, 1024], P(('groups', 'row'), 'col'), parts along dimension 0
- grad_queries: bfloat16 [4096, 1024], P(('groups', 'row'), 'col'), parts along dimension 0
- grad_keys: bfloat16 [4096, 1024], P(('groups', 'col'), 'row'), parts along dimension 0
- grad_values: bfloat16 [4096, 1024], P(('groups', 'col'), 'row'), parts along dimension 0
There are 2 independent parts, one for each index of `groups`. A program takes and returns all parts, laid end to end along the dimension named above; each array names one. Nothing has to cross between parts.
Inputs may be any that keep to these rules, and one draw needn't show every extreme that they name: `block_lists`: each row lists 16 distinct blocks; its first entry is the query block itself. `block_counts`: some query block has all 16 entries live in every draw.
All inputs are finite; a program needn't handle non-finite values.
Results may differ from a plain program's by a relative error of at most 0.011.
Values may be sent and summed in bfloat16 or wider, within the bound.
No kernel may reach another device: no remote copies, remote signals or barrier semaphores. Data moves between devices by JAX's collectives and lax.ppermute only.
A program may use at most 64 MiB of HBM per device.

v0:
```python
import math

import jax
import jax.numpy as jnp
from jax import lax
from jax.sharding import PartitionSpec as P

D = 1024
HEADS = 16
HEAD = 64
BLK = 128
MAXNB = 16


NEG_FILL = -1e30


def tile_scores(query_tile, key_tile, score_scale):
    query_heads = query_tile.reshape(query_tile.shape[0], HEADS, -1)
    key_heads = key_tile.reshape(key_tile.shape[0], HEADS, -1)
    return (
        jnp.einsum("qhd,khd->hqk", query_heads, key_heads, preferred_element_type=jnp.float32)
        * score_scale
    )


def on_device(queries, keys, values, cotangent, block_lists, block_counts):
    score_scale = 1.0 / math.sqrt(HEAD)
    q_full = lax.all_gather(queries, "col", axis=1, tiled=True)
    k_full, v_full = (
        lax.all_gather(keys, "row", axis=1, tiled=True),
        lax.all_gather(values, "row", axis=1, tiled=True),
    )
    q_rows = q_full.shape[0]
    k_rows = k_full.shape[0]
    q_blocks = q_rows // BLK
    k_blocks = k_rows // BLK
    group_size = min(4, q_blocks)
    span_rows = group_size * BLK
    supers = q_blocks // group_size
    tile_count = supers * k_blocks
    first_key = lax.axis_index("col") * k_blocks
    wanted = first_key + jnp.arange(k_blocks, dtype=jnp.int32)
    live_slots = jnp.arange(MAXNB, dtype=jnp.int32)[None, :] < block_counts[:, None]
    block_hit = jnp.any(
        (block_lists[:, :, None] == wanted[None, None, :]) & live_slots[:, :, None], axis=1
    )
    block_hit = block_hit.reshape(supers, group_size, k_blocks).transpose(0, 2, 1)
    row_mask = jnp.repeat(block_hit, BLK, axis=2)
    tile_any = jnp.any(block_hit, axis=2)

    def tile_parts(step):
        super_at = step // k_blocks
        key_at = step % k_blocks
        query_tile = lax.dynamic_slice_in_dim(q_full, super_at * span_rows, span_rows, 0)
        key_tile = lax.dynamic_slice_in_dim(k_full, key_at * BLK, BLK, 0)
        value_tile = lax.dynamic_slice_in_dim(v_full, key_at * BLK, BLK, 0)
        keep_mask = row_mask[super_at, key_at][None, :, None]
        return (super_at, key_at, query_tile, key_tile, value_tile, keep_mask)

    def unchanged(carry):
        return carry

    def stats_step(step, carry):
        super_at, key_at, query_tile, key_tile, value_tile, keep_mask = tile_parts(step)

        def stats_work(state):
            row_top, row_total = state
            scores = jnp.where(keep_mask, tile_scores(query_tile, key_tile, score_scale), NEG_FILL)
            old_top = lax.dynamic_slice_in_dim(row_top, super_at * span_rows, span_rows, 1)
            old_total = lax.dynamic_slice_in_dim(row_total, super_at * span_rows, span_rows, 1)
            new_top = jnp.maximum(old_top, jnp.max(scores, axis=2))
            exp_terms = jnp.where(keep_mask, jnp.exp(scores - new_top[:, :, None]), 0.0)
            fresh = old_total * jnp.exp(old_top - new_top) + jnp.sum(exp_terms, axis=2)
            return (
                lax.dynamic_update_slice_in_dim(row_top, new_top, super_at * span_rows, 1),
                lax.dynamic_update_slice_in_dim(row_total, fresh, super_at * span_rows, 1),
            )

        return lax.cond(tile_any[super_at, key_at], stats_work, unchanged, carry)

    start_top = jnp.full((HEADS, q_rows), NEG_FILL, jnp.float32)
    start_total = jnp.zeros((HEADS, q_rows), jnp.float32)
    local_top, local_total = lax.fori_loop(0, tile_count, stats_step, (start_top, start_total))
    row_top = lax.pmax(local_top.astype(jnp.bfloat16), "col").astype(local_top.dtype)
    row_total = lax.psum(local_total * jnp.exp(local_top - row_top), "col")

    def tile_weights(scores, super_at, keep_mask):
        top_rows = lax.dynamic_slice_in_dim(row_top, super_at * span_rows, span_rows, 1)
        total_rows = lax.dynamic_slice_in_dim(row_total, super_at * span_rows, span_rows, 1)
        ratio = jnp.exp(scores - top_rows[:, :, None]) / total_rows[:, :, None]
        return jnp.where(keep_mask, ratio, 0.0).astype(jnp.bfloat16)

    def output_step(step, carry):
        super_at, key_at, query_tile, key_tile, value_tile, keep_mask = tile_parts(step)

        def output_work(out_rows):
            scores = jnp.where(keep_mask, tile_scores(query_tile, key_tile, score_scale), NEG_FILL)
            weights = tile_weights(scores, super_at, keep_mask)
            value_heads = value_tile.reshape(BLK, HEADS, -1)
            part = jnp.einsum(
                "hqk,khd->qhd", weights, value_heads, preferred_element_type=jnp.float32
            ).reshape(span_rows, -1)
            current = lax.dynamic_slice_in_dim(out_rows, super_at * span_rows, span_rows, 0)
            return lax.dynamic_update_slice_in_dim(
                out_rows, current + part, super_at * span_rows, 0
            )

        return lax.cond(tile_any[super_at, key_at], output_work, unchanged, carry)

    partial_out = lax.fori_loop(0, tile_count, output_step, jnp.zeros((q_rows, D), jnp.float32))
    out_share = lax.psum_scatter(partial_out, "col", scatter_dimension=1, tiled=True).astype(
        jnp.bfloat16
    )
    grad_full, out_full = (
        lax.all_gather(cotangent, "col", axis=1, tiled=True),
        lax.all_gather(out_share, "col", axis=1, tiled=True),
    )
    delta = jnp.einsum(
        "qhd,qhd->hq",
        grad_full.reshape(q_rows, HEADS, -1),
        out_full.reshape(q_rows, HEADS, -1),
        preferred_element_type=jnp.float32,
    )

    def grad_step(step, carry):
        super_at, key_at, query_tile, key_tile, value_tile, keep_mask = tile_parts(step)

        def grad_work(state):
            query_accum, key_accum, value_accum = state
            scores = jnp.where(keep_mask, tile_scores(query_tile, key_tile, score_scale), NEG_FILL)
            weights = tile_weights(scores, super_at, keep_mask)
            grad_tile = lax.dynamic_slice_in_dim(
                grad_full, super_at * span_rows, span_rows, 0
            ).reshape(span_rows, HEADS, -1)
            value_heads = value_tile.reshape(BLK, HEADS, -1)
            key_heads = key_tile.reshape(BLK, HEADS, -1)
            query_heads = query_tile.reshape(span_rows, HEADS, -1)
            dweights = jnp.einsum(
                "qhd,khd->hqk", grad_tile, value_heads, preferred_element_type=jnp.float32
            )
            delta_rows = lax.dynamic_slice_in_dim(delta, super_at * span_rows, span_rows, 1)
            dscores = (weights.astype(jnp.float32) * (dweights - delta_rows[:, :, None])).astype(
                jnp.bfloat16
            )
            query_part = score_scale * jnp.einsum(
                "hqk,khd->qhd", dscores, key_heads, preferred_element_type=jnp.float32
            )
            key_part = score_scale * jnp.einsum(
                "hqk,qhd->khd", dscores, query_heads, preferred_element_type=jnp.float32
            )
            value_part = jnp.einsum(
                "hqk,qhd->khd", weights, grad_tile, preferred_element_type=jnp.float32
            )
            query_now = lax.dynamic_slice_in_dim(query_accum, super_at * span_rows, span_rows, 0)
            key_now = lax.dynamic_slice_in_dim(key_accum, key_at * BLK, BLK, 0)
            value_now = lax.dynamic_slice_in_dim(value_accum, key_at * BLK, BLK, 0)
            query_accum = lax.dynamic_update_slice_in_dim(
                query_accum, query_now + query_part.reshape(span_rows, -1), super_at * span_rows, 0
            )
            key_accum = lax.dynamic_update_slice_in_dim(
                key_accum, key_now + key_part.reshape(BLK, -1), key_at * BLK, 0
            )
            value_accum = lax.dynamic_update_slice_in_dim(
                value_accum, value_now + value_part.reshape(BLK, -1), key_at * BLK, 0
            )
            return (query_accum, key_accum, value_accum)

        return lax.cond(tile_any[super_at, key_at], grad_work, unchanged, carry)

    start_grads = (
        jnp.zeros((q_rows, D), jnp.float32),
        jnp.zeros((k_rows, D), jnp.float32),
        jnp.zeros((k_rows, D), jnp.float32),
    )
    query_parts, key_parts, value_parts = lax.fori_loop(0, tile_count, grad_step, start_grads)
    grad_queries = lax.psum_scatter(query_parts, "col", scatter_dimension=1, tiled=True).astype(
        jnp.bfloat16
    )
    grad_keys, grad_values = (
        lax.psum_scatter(key_parts, "row", scatter_dimension=1, tiled=True),
        lax.psum_scatter(value_parts, "row", scatter_dimension=1, tiled=True),
    )
    return (
        out_share,
        grad_queries,
        grad_keys.astype(jnp.bfloat16),
        grad_values.astype(jnp.bfloat16),
    )


def solution(mesh):
    return jax.shard_map(
        on_device,
        mesh=mesh,
        in_specs=(
            P(("groups", "row"), "col"),
            P(("groups", "col"), "row"),
            P(("groups", "col"), "row"),
            P(("groups", "row"), "col"),
            P(("groups", "row"), None),
            P(("groups", "row")),
        ),
        out_specs=(
            P(("groups", "row"), "col"),
            P(("groups", "row"), "col"),
            P(("groups", "col"), "row"),
            P(("groups", "col"), "row"),
        ),
        check_vma=False,
    )
```

profile of v0, /device:TPU:0, one launch (start us, length us, event | category | flops | bytes accessed | tf_op | source)
XLA Modules:
  0.0 402.9 jit_solution(14908098541145584658)
XLA Ops:
  7.2 1.8 copy.31
  9.1 1.8 copy.30
  11.0 1.8 copy.33
  13.3 16.3 %all-gather.8.cloned.1.call-done = bf16[512,1024]{0,1:T(8,128)(2,1)} async-done(((bf16[512,256]{0,1:T(8,128)(2,1)}), bf16[512,1024]{0,1:T(8,128)(2,1)}) %all-gather.8.cloned.1.call-update) | async-done | bytes 1048592 | tf_op jit(solution)/shard_map/all_gather | solution.py:29
  29.6 30.1 %all-gather.6.cloned.1.call-done = bf16[512,1024]{0,1:T(8,128)(2,1)} async-done(((bf16[512,256]{0,1:T(8,128)(2,1)}), bf16[512,1024]{0,1:T(8,128)(2,1)}) %all-gather.6.cloned.1.call-update) | async-done | bytes 1048592 | tf_op jit(solution)/shard_map/all_gather | solution.py:31
  59.7 21.9 %while.57 = (s32[]{:T(128)}, f32[16,512]{1,0:T(8,128)S(1)}, f32[16,512]{1,0:T(8,128)S(1)}, pred[1,4]{1,0:T(4,128)(4,1)S(1)}, bf16[512,1024]{0,1:T(8,128)(2,1)}, ...) while((s32[]{:T(128)}, f32[16,512]{1,0:T(8,128)S(1)}, ...), condition=%wide.region_7.8_spmd.clone, body=%wide.region_2.7_spmd.clone.sunk | while | flops 142622736 | bytes 10658168 | solution.py:84
  60.3 4.8 %conditional.9 = ((f32[16,512]{1,0:T(8,128)S(1)}, f32[16,512]{1,0:T(8,128)S(1)})) conditional(s32[]{:T(128)} %bitcast.68, (f32[16,512]{1,0:T(8,128)S(1)}, f32[16,512]{1,0:T(8,128)S(1)}) %tuple.194, (pred[4,4]{1,0:T(4,128)(4,1)S(1)}, s32[]{:T(128)}, s32[]{:T(128)}, bf16[512,1024]{0,1:T(8,128)(2,1)}, bf16[512,1024]{0,1:T(8,128)(2,1)}, ...), branch_computations={%region_3.3_spmd, %region_4.6_spmd} | conditional | flops 142622720 | bytes 10657886 | solution.py:80
  62.1 2.0 bitcast_reduce_fusion
  65.8 4.9 %conditional.9 = ((f32[16,512]{1,0:T(8,128)S(1)}, f32[16,512]{1,0:T(8,128)S(1)})) conditional(s32[]{:T(128)} %bitcast.68, (f32[16,512]{1,0:T(8,128)S(1)}, f32[16,512]{1,0:T(8,128)S(1)}) %tuple.194, (pred[4,4]{1,0:T(4,128)(4,1)S(1)}, s32[]{:T(128)}, s32[]{:T(128)}, bf16[512,1024]{0,1:T(8,128)(2,1)}, bf16[512,1024]{0,1:T(8,128)(2,1)}, ...), branch_computations={%region_3.3_spmd, %region_4.6_spmd} | conditional | flops 142622720 | bytes 10657886 | solution.py:80
  67.5 2.0 bitcast_reduce_fusion
  71.3 4.8 %conditional.9 = ((f32[16,512]{1,0:T(8,128)S(1)}, f32[16,512]{1,0:T(8,128)S(1)})) conditional(s32[]{:T(128)} %bitcast.68, (f32[16,512]{1,0:T(8,128)S(1)}, f32[16,512]{1,0:T(8,128)S(1)}) %tuple.194, (pred[4,4]{1,0:T(4,128)(4,1)S(1)}, s32[]{:T(128)}, s32[]{:T(128)}, bf16[512,1024]{0,1:T(8,128)(2,1)}, bf16[512,1024]{0,1:T(8,128)(2,1)}, ...), branch_computations={%region_3.3_spmd, %region_4.6_spmd} | conditional | flops 142622720 | bytes 10657886 | solution.py:80
  73.0 2.0 bitcast_reduce_fusion
  76.8 4.8 %conditional.9 = ((f32[16,512]{1,0:T(8,128)S(1)}, f32[16,512]{1,0:T(8,128)S(1)})) conditional(s32[]{:T(128)} %bitcast.68, (f32[16,512]{1,0:T(8,128)S(1)}, f32[16,512]{1,0:T(8,128)S(1)}) %tuple.194, (pred[4,4]{1,0:T(4,128)(4,1)S(1)}, s32[]{:T(128)}, s32[]{:T(128)}, bf16[512,1024]{0,1:T(8,128)(2,1)}, bf16[512,1024]{0,1:T(8,128)(2,1)}, ...), branch_computations={%region_3.3_spmd, %region_4.6_spmd} | conditional | flops 142622720 | bytes 10657886 | solution.py:80
  78.5 2.0 bitcast_reduce_fusion
  81.6 10.7 %pmax.7 = bf16[16,512]{1,0:T(8,128)(2,1)S(1)} all-reduce(bf16[16,512]{1,0:T(8,128)(2,1)S(1)} %convert_element_type.89), channel_id=1, replica_groups=mesh['groups'=2,'row'=4,'col'=4] {'col'}, use_global_device_ids=true, to_apply=%region_8.9 | all-reduce | flops 8192 | bytes 32768 | tf_op jit(solution)/shard_map/pmax | solution.py:85
  92.3 10.3 %psum.7 = f32[16,512]{1,0:T(8,128)S(1)} all-reduce(f32[16,512]{1,0:T(8,128)S(1)} %exponential_multiply_fusion), channel_id=1, replica_groups=mesh['groups'=2,'row'=4,'col'=4] {'col'}, use_global_device_ids=true, to_apply=%region_9.10 | all-reduce | flops 8192 | bytes 65536 | tf_op jit(solution)/shard_map/psum | solution.py:86
  102.9 36.9 %while.58 = (s32[]{:T(128)}, f32[512,1024]{0,1:T(8,128)S(1)}, pred[1,4]{1,0:T(4,128)(4,1)S(1)}, bf16[512,1024]{0,1:T(8,128)(2,1)}, bf16[512,1024]{0,1:T(8,128)(2...) while((s32[]{:T(128)}, f32[512,1024]{0,1:T(8,128)S(1)}, ...), condition=%wide.region_13.14_spmd.clone, body=%wide.region_10.13_spmd.clone.sunk | while | flops 275251200 | bytes 11083640 | solution.py:111
  103.6 8.6 %conditional.10 = (f32[512,1024]{0,1:T(8,128)S(1)}) conditional(s32[]{:T(128)} %bitcast.69, f32[512,1024]{0,1:T(8,128)S(1)} %get-tuple-element.1617, (pred[4,4]{1,0:T(4,128)(4,1)S(1)}, s32[]{:T(128)}, s32[]{:T(128)}, bf16[512,1024]{0,1:T(8,128)(2,1)}, bf16[512,1024]{0,1:T(8,128)(2,1)S(1)}, /*index=5*/f32[16,512]{1,0:T(8,128)S(1)}, ...), branch_computations={%region_11.11_spmd, %region_12.12_spmd} | conditional | flops 275251200 | bytes 11083342 | solution.py:109
  104.4 1.8 constant_dynamic-slice_fusion.2
  106.2 3.8 fusion.9
  110.0 2.1 bitcast_add_fusion
  112.8 8.6 %conditional.10 = (f32[512,1024]{0,1:T(8,128)S(1)}) conditional(s32[]{:T(128)} %bitcast.69, f32[512,1024]{0,1:T(8,128)S(1)} %get-tuple-element.1617, (pred[4,4]{1,0:T(4,128)(4,1)S(1)}, s32[]{:T(128)}, s32[]{:T(128)}, bf16[512,1024]{0,1:T(8,128)(2,1)}, bf16[512,1024]{0,1:T(8,128)(2,1)S(1)}, /*index=5*/f32[16,512]{1,0:T(8,128)S(1)}, ...), branch_computations={%region_11.11_spmd, %region_12.12_spmd} | conditional | flops 275251200 | bytes 11083342 | solution.py:109
  113.6 1.8 constant_dynamic-slice_fusion.2
  115.4 3.8 fusion.9
  119.2 2.1 bitcast_add_fusion
  122.0 8.6 %conditional.10 = (f32[512,1024]{0,1:T(8,128)S(1)}) conditional(s32[]{:T(128)} %bitcast.69, f32[512,1024]{0,1:T(8,128)S(1)} %get-tuple-element.1617, (pred[4,4]{1,0:T(4,128)(4,1)S(1)}, s32[]{:T(128)}, s32[]{:T(128)}, bf16[512,1024]{0,1:T(8,128)(2,1)}, bf16[512,1024]{0,1:T(8,128)(2,1)S(1)}, /*index=5*/f32[16,512]{1,0:T(8,128)S(1)}, ...), branch_computations={%region_11.11_spmd, %region_12.12_spmd} | conditional | flops 275251200 | bytes 11083342 | solution.py:109
  122.8 1.8 constant_dynamic-slice_fusion.2
  124.6 3.8 fusion.9
  128.4 2.1 bitcast_add_fusion
  131.2 8.6 %conditional.10 = (f32[512,1024]{0,1:T(8,128)S(1)}) conditional(s32[]{:T(128)} %bitcast.69, f32[512,1024]{0,1:T(8,128)S(1)} %get-tuple-element.1617, (pred[4,4]{1,0:T(4,128)(4,1)S(1)}, s32[]{:T(128)}, s32[]{:T(128)}, bf16[512,1024]{0,1:T(8,128)(2,1)}, bf16[512,1024]{0,1:T(8,128)(2,1)S(1)}, /*index=5*/f32[16,512]{1,0:T(8,128)S(1)}, ...), branch_computations={%region_11.11_spmd, %region_12.12_spmd} | conditional | flops 275251200 | bytes 11083342 | solution.py:109
  132.1 1.8 constant_dynamic-slice_fusion.2
  133.8 3.8 fusion.9
  137.7 2.1 bitcast_add_fusion
  142.1 30.3 %reduce-scatter.5.cloned.1.call-done = f32[512,256]{0,1:T(8,128)} async-done(((f32[512,1024]{0,1:T(8,128)}), f32[512,256]{0,1:T(8,128)}) %reduce-scatter.5.cloned.1.call-update) | async-done | bytes 524304 | tf_op jit(solution)/shard_map/reduce_scatter | solution.py:112
  172.4 1.8 convert_element_type.91
  174.3 17.0 %all-gather.12.cloned.1.call-done = bf16[512,1024]{0,1:T(8,128)(2,1)} async-done(((bf16[512,256]{0,1:T(8,128)(2,1)}), bf16[512,1024]{0,1:T(8,128)(2,1)}) %all-gather.12.cloned.1.call-update) | async-done | bytes 1048592 | tf_op jit(solution)/shard_map/all_gather | solution.py:116
  191.3 18.8 %all-gather.14.cloned.1.call-done = bf16[512,1024]{0,1:T(8,128)(2,1)} async-done(((bf16[512,256]{0,1:T(8,128)(2,1)}), bf16[512,1024]{0,1:T(8,128)(2,1)}) %all-gather.14.cloned.1.call-update) | async-done | bytes 1048592 | tf_op jit(solution)/shard_map/all_gather | solution.py:117
  210.1 1.9 fusion.13
  212.0 1.6 broadcast.97.clone.2
  213.6 1.6 broadcast.97.clone.1
  215.2 1.6 broadcast.97
  216.8 51.4 %while.59 = (s32[]{:T(128)}, f32[512,1024]{0,1:T(8,128)}, f32[512,1024]{0,1:T(8,128)}, f32[512,1024]{0,1:T(8,128)}, pred[1,4]{1,0:T(4,128)(4,1)S(1)}, /*index=5*...) while((s32[]{:T(128)}, f32[512,1024]{0,1:T(8,128)}, ...), condition=%wide.region_18.19_spmd.clone, body=%wide.region_15.18_spmd.clone.sunk | while | flops 683016192 | bytes 48078884 | solution.py:176
  217.4 12.3 %conditional.11 = ((f32[512,1024]{0,1:T(8,128)}, f32[512,1024]{0,1:T(8,128)}, f32[512,1024]{0,1:T(8,128)})) conditional(s32[]{:T(128)} %bitcast.70, (f32[512,1024]{0,1:T(8,128)}, f32[512,1024]{0,1:T(8,128)}, f32[512,1024]{0,1:T(8,128)}) %tuple.199, (pred[4,4]{1,0:T(4,128)(4,1)S(1)}, s32[]{:T(128)}, s32[]{:T(128)}, bf16[512,1024]{0,1:T(8,128)(2,1)}, ...), branch_computations={%region_16.16_spmd, %region_17.17_spmd} | conditional | flops 683016192 | bytes 48078500 | solution.py:169
  220.0 1.4 select_convert_fusion.1
  227.3 2.3 constant_dynamic-update-slice_fusion
  230.2 12.3 %conditional.11 = ((f32[512,1024]{0,1:T(8,128)}, f32[512,1024]{0,1:T(8,128)}, f32[512,1024]{0,1:T(8,128)})) conditional(s32[]{:T(128)} %bitcast.70, (f32[512,1024]{0,1:T(8,128)}, f32[512,1024]{0,1:T(8,128)}, f32[512,1024]{0,1:T(8,128)}) %tuple.199, (pred[4,4]{1,0:T(4,128)(4,1)S(1)}, s32[]{:T(128)}, s32[]{:T(128)}, bf16[512,1024]{0,1:T(8,128)(2,1)}, ...), branch_computations={%region_16.16_spmd, %region_17.17_spmd} | conditional | flops 683016192 | bytes 48078500 | solution.py:169
  232.9 1.4 select_convert_fusion.1
  240.1 2.4 constant_dynamic-update-slice_fusion
  243.1 12.3 %conditional.11 = ((f32[512,1024]{0,1:T(8,128)}, f32[512,1024]{0,1:T(8,128)}, f32[512,1024]{0,1:T(8,128)})) conditional(s32[]{:T(128)} %bitcast.70, (f32[512,1024]{0,1:T(8,128)}, f32[512,1024]{0,1:T(8,128)}, f32[512,1024]{0,1:T(8,128)}) %tuple.199, (pred[4,4]{1,0:T(4,128)(4,1)S(1)}, s32[]{:T(128)}, s32[]{:T(128)}, bf16[512,1024]{0,1:T(8,128)(2,1)}, ...), branch_computations={%region_16.16_spmd, %region_17.17_spmd} | conditional | flops 683016192 | bytes 48078500 | solution.py:169
  245.7 1.4 select_convert_fusion.1
  253.0 2.3 constant_dynamic-update-slice_fusion
  255.9 12.3 %conditional.11 = ((f32[512,1024]{0,1:T(8,128)}, f32[512,1024]{0,1:T(8,128)}, f32[512,1024]{0,1:T(8,128)})) conditional(s32[]{:T(128)} %bitcast.70, (f32[512,1024]{0,1:T(8,128)}, f32[512,1024]{0,1:T(8,128)}, f32[512,1024]{0,1:T(8,128)}) %tuple.199, (pred[4,4]{1,0:T(4,128)(4,1)S(1)}, s32[]{:T(128)}, s32[]{:T(128)}, bf16[512,1024]{0,1:T(8,128)(2,1)}, ...), branch_computations={%region_16.16_spmd, %region_17.17_spmd} | conditional | flops 683016192 | bytes 48078500 | solution.py:169
  265.8 2.4 constant_dynamic-update-slice_fusion
  268.2 2.9 copy.37
  271.2 1.5 copy-done.4
  272.7 1.8 copy.35
  274.6 1.5 copy-done.6
  276.1 1.8 copy.36
  279.7 35.3 %reduce-scatter.11.cloned.1.call-done = f32[512,256]{1,0:T(8,128)} async-done(((f32[512,1024]{1,0:T(8,128)}), f32[512,256]{1,0:T(8,128)}) %reduce-scatter.11.cloned.1.call-update) | async-done | bytes 524304 | tf_op jit(solution)/shard_map/reduce_scatter | solution.py:182
  315.0 1.8 convert_element_type.94
  316.8 31.5 %reduce-scatter.7.cloned.1.call-done = f32[512,256]{1,0:T(8,128)} async-done(((f32[512,1024]{1,0:T(8,128)}), f32[512,256]{1,0:T(8,128)}) %reduce-scatter.7.cloned.1.call-update) | async-done | bytes 524304 | tf_op jit(solution)/shard_map/reduce_scatter | solution.py:177
  348.3 1.8 convert_element_type.92
  350.1 44.5 %reduce-scatter.9.cloned.1.call-done = f32[512,256]{1,0:T(8,128)} async-done(((f32[512,1024]{1,0:T(8,128)}), f32[512,256]{1,0:T(8,128)}) %reduce-scatter.9.cloned.1.call-update) | async-done | bytes 524304 | tf_op jit(solution)/shard_map/reduce_scatter | solution.py:181
  394.6 1.8 convert_element_type.93
  (160 shorter events, 54.6 us)
Async XLA Ops:
  7.2 5.7 %copy-start.10 = (s32[4]{0:T(128)S(1)}, s32[4]{0:T(128)}, u32[]{:S(2)}) copy-start(s32[4]{0:T(128)} %param.23) | copy-start | bytes 52
  7.2 5.8 %copy-start.9 = (s32[4,16]{1,0:T(4,128)S(1)}, s32[4,16]{1,0:T(4,128)}, u32[]{:S(2)}) copy-start(s32[4,16]{1,0:T(4,128)} %param.22) | copy-start | bytes 772
  7.2 22.4 %all-gather.8.cloned.1.call-start = ((), (), s32[]{:S(2)}) async-start(), calls=%async_computation.5 | async-start | bytes 1310720 | tf_op jit(solution)/shard_map/all_gather | solution.py:29
  9.1 50.7 %all-gather.6.cloned.1.call-start = ((), (), s32[]{:S(2)}) async-start(), calls=%async_computation.4 | async-start | bytes 1310720 | tf_op jit(solution)/shard_map/all_gather | solution.py:31
  10.9 91.7 %all-gather.10.cloned.1.call-start = ((), (), s32[]{:S(2)}) async-start(), calls=%async_computation.6 | async-start | bytes 1310720 | tf_op jit(solution)/shard_map/all_gather | solution.py:32
  12.8 159.7 %reduce-scatter.5.cloned.1.call-start = ((), (), s32[]{:S(2)}) async-start(), calls=%async_computation.7 | async-start | bytes 2621440 | tf_op jit(solution)/shard_map/reduce_scatter | solution.py:112
  81.6 21.3 %copy-start.1 = (bf16[512,1024]{0,1:T(8,128)(2,1)S(1)}, bf16[512,1024]{0,1:T(8,128)(2,1)}, u32[]{:S(2)}) copy-start(bf16[512,1024]{0,1:T(8,128)(2,1)} %get-tuple-element.1707) | copy-start | bytes 3145732
  139.8 1.3 copy-start.5
  139.8 1.4 copy-start.8
  141.2 50.1 %all-gather.12.cloned.1.call-start = ((), (), s32[]{:S(2)}) async-start(), calls=%async_computation.8 | async-start | bytes 1310720 | tf_op jit(solution)/shard_map/all_gather | solution.py:116
  142.1 68.0 %all-gather.14.cloned.1.call-start = ((), (), s32[]{:S(2)}) async-start(), calls=%async_computation.9 | async-start | bytes 1310720 | tf_op jit(solution)/shard_map/all_gather | solution.py:117
  174.2 140.8 %reduce-scatter.11.cloned.1.call-start = ((), (), s32[]{:S(2)}) async-start(), calls=%async_computation.12 | async-start | bytes 2621440 | tf_op jit(solution)/shard_map/reduce_scatter | solution.py:182
  213.6 3.2 copy-start
  223.8 1.6 copy-start.2
  226.0 1.3 copy-start.3
  236.7 1.6 copy-start.2
  238.8 1.3 copy-start.3
  249.5 1.6 copy-start.2
  251.7 1.3 copy-start.3
  262.4 1.6 copy-start.2
  264.5 1.3 copy-start.3
  271.1 1.6 copy-start.4
  271.1 77.2 %reduce-scatter.7.cloned.1.call-start = ((), (), s32[]{:S(2)}) async-start(), calls=%async_computation.10 | async-start | bytes 2621440 | tf_op jit(solution)/shard_map/reduce_scatter | solution.py:177
  274.5 1.6 copy-start.6
  274.5 120.1 %reduce-scatter.9.cloned.1.call-start = ((), (), s32[]{:S(2)}) async-start(), calls=%async_computation.11 | async-start | bytes 2621440 | tf_op jit(solution)/shard_map/reduce_scatter | solution.py:181
  278.0 0.9 copy-start.7
Sparse Core Ops, SparseCore 0:
  10.2 19.4 all-gather.7
  31.7 27.9 all-gather.5
  61.9 27.3 all-gather.9
  141.3 31.1 reduce-scatter.4
  174.5 16.7 all-gather.11
  193.3 16.7 all-gather.13
  271.2 43.7 reduce-scatter.10
  317.5 30.7 reduce-scatter.6
  350.7 43.8 reduce-scatter.8
where the time goes:
time: 405 us; the launch traced here: 403 us
  waiting for transfers between devices  224 us (55%)
  local copies, waits for them, and re-layouts  54.1 us (13%)
  other arithmetic  41 us (10%)
  matrix products  40.2 us (10%)
  blocking collectives  20.9 us (5%)
  between operations  14 us (3%)
  loops' own time  8.26 us (2%)
    reduce_scatter x1, waiting for transfers between devices, on_device(): lax.psum_scatter(key_parts, 'row', scatter_dimension=1, tiled=True)  44.5 us
    reduce_scatter x1, waiting for transfers between devices, on_device(): lax.psum_scatter(value_parts, 'row', scatter_dimension=1, tiled=True)  35.3 us
    reduce_scatter x1, waiting for transfers between devices, on_device(): lax.psum_scatter(query_parts, 'col', scatter_dimension=1, tiled=True)  31.5 us
    reduce_scatter x1, waiting for transfers between devices, on_device(): lax.psum_scatter(partial_out, 'col', scatter_dimension=1, tiled=True)  30.3 us
    all_gather x1, waiting for transfers between devices, on_device(): lax.all_gather(keys, 'row', axis=1, tiled=True)  30.1 us
    all_gather x1, waiting for transfers between devices, on_device(): lax.all_gather(out_share, 'col', axis=1, tiled=True)  18.8 us
    all_gather x1, waiting for transfers between devices, on_device(): lax.all_gather(cotangent, 'col', axis=1, tiled=True)  17 us
    all_gather x1, waiting for transfers between devices, on_device(): q_full = lax.all_gather(queries, 'col', axis=1, tiled=True)  16.3 us
  transfers between devices with their start and end apart: 9, of which 8 were waited for; matrix products, arithmetic and copies ran while one was open for 8% of the time, Pallas kernels for 0%

commit v1 on v0

--- a/solution.py
+++ b/solution.py
@@ -3,6 +3,8 @@
 import jax
 import jax.numpy as jnp
 from jax import lax
+from jax.experimental import pallas as pl
+from jax.experimental.pallas import tpu as pltpu
 from jax.sharding import PartitionSpec as P
 
 D = 1024
@@ -13,6 +15,214 @@
 
 
 NEG_FILL = -1e30
+GROUP = 2
+VMEM = pl.BlockSpec(memory_space=pltpu.VMEM)
+SMEM = pl.BlockSpec(memory_space=pltpu.SMEM)
+
+
+def pack_body(place, q_ref, g_ref, k_ref, v_ref, *outs):
+    chunks = q_ref.shape[1] // HEAD
+
+    def pack(left_ref, right_ref, out_refs, at):
+        for step in range(chunks):
+            head = (at + step) % chunks
+            lanes = slice(head * HEAD, (head + 1) * HEAD)
+            out_refs[step][...] = jnp.concatenate([left_ref[:, lanes], right_ref[:, lanes]], axis=1)
+
+    for at in range(chunks):
+
+        @pl.when(place[1] == at)
+        def _():
+            pack(k_ref, v_ref, outs[chunks:], at)
+
+        @pl.when(place[0] == at)
+        def _():
+            pack(q_ref, g_ref, outs[:chunks], at)
+
+
+def unpack_body(place, *refs):
+    left_ref, right_ref = refs[-2:]
+    chunks = len(refs) - 2
+    for at in range(chunks):
+
+        @pl.when(place[0] == at)
+        def _():
+            parts = [refs[(head - at) % chunks][...] for head in range(chunks)]
+            left_ref[...] = jnp.concatenate([p[:, :HEAD] for p in parts], axis=1)
+            right_ref[...] = jnp.concatenate([p[:, HEAD:] for p in parts], axis=1)
+
+
+def attend_body(q_blocks, last, table, x_ref, *refs):
+    kv_count = 4
+    kv_refs = refs[:kv_count]
+    acc_in = refs[kv_count]
+    og_ref, acc_ref, kv_all, kvt, tiles = refs[kv_count + 1 :]
+    scale = 1.0 / math.sqrt(HEAD)
+    to_log2 = scale * math.log2(math.e)
+    rows = kv_refs[0].shape[0]
+    per_chunk = rows // BLK
+
+    for part in range(kv_count):
+        kv_all[part * rows : (part + 1) * rows, :] = kv_refs[part][...]
+        for b in range(per_chunk):
+            lanes = slice((part * per_chunk + b) * BLK, (part * per_chunk + b + 1) * BLK)
+            kvt[:, lanes] = kv_refs[part][b * BLK : (b + 1) * BLK, :].T
+    acc_ref[...] = acc_in[...]
+    lane = lax.broadcasted_iota(jnp.int32, (BLK, 2 * HEAD), 1)
+    is_left = lane < HEAD
+
+    def fold(x, op):
+        return op(x.reshape(x.shape[0] // 8, 8, x.shape[1]), axis=0)
+
+    def query_block(qb, _):
+        count = table[qb, MAXNB]
+        groups = (count + GROUP - 1) // GROUP
+        x = x_ref[pl.ds(pl.multiple_of(qb * BLK, BLK), BLK), :]
+        zero = jnp.zeros_like(x)
+        both = jnp.concatenate([jnp.where(is_left, x, zero), jnp.where(is_left, zero, x)], axis=0)
+
+        def slot(at):
+            return pl.multiple_of(table[qb, jnp.minimum(at, MAXNB - 1)] * BLK, BLK)
+
+        def score_step(g, top):
+            for u in range(GROUP):
+                at = g * GROUP + u
+                kv = kv_all[pl.ds(slot(at), BLK), :]
+                st = lax.dot_general(
+                    kv, both, (((1,), (1,)), ((), ())), preferred_element_type=jnp.float32
+                )
+                bias = jnp.where(at < count, 0.0, NEG_FILL)
+                score = st[:, :BLK] * to_log2 + bias
+                tiles[at, :, :BLK] = score
+                tiles[at, :, BLK:] = st[:, BLK:]
+                top = jnp.maximum(top, fold(score, jnp.max))
+            return top
+
+        top = lax.fori_loop(0, groups, score_step, jnp.full((8, BLK), NEG_FILL, jnp.float32))
+        top = jnp.max(top, axis=0, keepdims=True)
+
+        def exp_step(g, carry):
+            total, dot = carry
+            for u in range(GROUP):
+                at = g * GROUP + u
+                e = jnp.exp2(tiles[at, :, :BLK] - top)
+                tiles[at, :, :BLK] = e
+                total = total + fold(e, jnp.sum)
+                dot = dot + fold(e * tiles[at, :, BLK:], jnp.sum)
+            return total, dot
+
+        zeros = jnp.zeros((8, BLK), jnp.float32)
+        total, dot = lax.fori_loop(0, groups, exp_step, (zeros, zeros))
+        inverse = 1.0 / jnp.sum(total, axis=0, keepdims=True)
+        delta = jnp.sum(dot, axis=0, keepdims=True) * inverse
+
+        def grad_step(g, out):
+            for u in range(GROUP):
+                at = g * GROUP + u
+                w = tiles[at, :, :BLK] * inverse
+                ds = (w * (tiles[at, :, BLK:] - delta)).astype(jnp.bfloat16)
+                w = w.astype(jnp.bfloat16)
+                start = slot(at)
+                acc_ref[pl.ds(start, BLK), :] += jnp.dot(
+                    jnp.concatenate([ds, w], axis=1), both, preferred_element_type=jnp.float32
+                )
+                t = kvt[:, pl.ds(start, BLK)]
+                out = out + jnp.concatenate(
+                    [
+                        jnp.dot(t[HEAD:, :], w, preferred_element_type=jnp.float32),
+                        jnp.dot(t[:HEAD, :], ds, preferred_element_type=jnp.float32) * scale,
+                    ],
+                    axis=0,
+                )
+            return out
+
+        out = lax.fori_loop(0, groups, grad_step, jnp.zeros((2 * HEAD, BLK), jnp.float32))
+        og_ref[pl.ds(pl.multiple_of(qb * BLK, BLK), BLK), :] = out.T.astype(og_ref.dtype)
+        return 0
+
+    lax.fori_loop(0, q_blocks, query_block, 0)
+
+
+def gkv_round(acc, chunks):
+    scale = 1.0 / math.sqrt(HEAD)
+    lane = lax.broadcasted_iota(jnp.int32, acc.shape, 1)
+    out = jnp.where(lane < HEAD, acc * scale, acc).astype(jnp.bfloat16)
+    return out.reshape(chunks, -1, 2 * HEAD)
+
+
+def head_per_device(queries, keys, values, cotangent, block_lists, block_counts):
+    chunks = 4
+    rows = queries.shape[0]
+    q_blocks = rows // BLK
+    at_row, at_col = lax.axis_index("row"), lax.axis_index("col")
+    place = jnp.stack([at_row, at_col]).astype(jnp.int32)
+    chunk = jax.ShapeDtypeStruct((rows, 2 * HEAD), jnp.bfloat16)
+    packed = pl.pallas_call(
+        pack_body,
+        out_shape=[chunk] * (2 * chunks),
+        in_specs=[SMEM] + [VMEM] * 4,
+        out_specs=[VMEM] * (2 * chunks),
+    )(place, queries, cotangent, keys, values)
+
+    table = jnp.concatenate([block_lists, block_counts[:, None]], axis=1)
+
+    def q_perm(step):
+        return [
+            (r * chunks + c, c * chunks + (r + step) % chunks)
+            for r in range(chunks)
+            for c in range(chunks)
+        ]
+
+    def k_perm(step):
+        return [(c, (c + step) % chunks) for c in range(chunks)]
+
+    def swap(perm):
+        return [(b, a) for a, b in perm]
+
+    axes = ("row", "col")
+    kv = [packed[chunks]] + [
+        lax.ppermute(packed[chunks + s], "col", k_perm(s)) for s in range(1, chunks)
+    ]
+    tables = [lax.ppermute(table, axes, q_perm(s)) for s in range(chunks)]
+    xs = [lax.ppermute(packed[s], axes, q_perm(s)) for s in range(chunks)]
+
+    acc = jnp.zeros((chunks * rows, 2 * HEAD), jnp.float32)
+    outs = []
+    for s in range(chunks):
+        own = tables[s]
+        block = own[:, :MAXNB]
+        part = (at_col - block // q_blocks) % chunks
+        slots = part * q_blocks + block % q_blocks
+        own = jnp.concatenate([slots, own[:, MAXNB:]], axis=1)
+        og, acc = pl.pallas_call(
+            lambda *refs: attend_body(q_blocks, s == chunks - 1, *refs),
+            out_shape=[chunk, jax.ShapeDtypeStruct(acc.shape, jnp.float32)],
+            in_specs=[SMEM] + [VMEM] * (2 + chunks),
+            out_specs=[VMEM, VMEM],
+            scratch_shapes=[
+                pltpu.VMEM((chunks * rows, 2 * HEAD), jnp.bfloat16),
+                pltpu.VMEM((2 * HEAD, chunks * rows), jnp.bfloat16),
+                pltpu.VMEM((MAXNB, BLK, 2 * BLK), jnp.float32),
+            ],
+            input_output_aliases={2 + chunks: 1},
+        )(own, xs[s], *kv, acc)
+        outs.append(lax.ppermute(og, axes, swap(q_perm(s))))
+    gkv = gkv_round(acc, chunks)
+    gkv = [gkv[0]] + [lax.ppermute(gkv[s], "col", swap(k_perm(s))) for s in range(1, chunks)]
+
+    whole = jax.ShapeDtypeStruct(queries.shape, jnp.bfloat16)
+
+    def unpack(at, parts):
+        return pl.pallas_call(
+            unpack_body,
+            out_shape=[whole, whole],
+            in_specs=[SMEM] + [VMEM] * chunks,
+            out_specs=[VMEM, VMEM],
+        )(jnp.reshape(at, (1,)).astype(jnp.int32), *parts)
+
+    attended, grad_queries = unpack(at_row, outs)
+    grad_keys, grad_values = unpack(at_col, gkv)
+    return attended, grad_queries, grad_keys, grad_values
 
 
 def tile_scores(query_tile, key_tile, score_scale):
@@ -190,8 +400,10 @@
 
 
 def solution(mesh):
+    rows, cols = mesh.shape["row"], mesh.shape["col"]
+    one_head = rows == 4 and cols == 4
     return jax.shard_map(
-        on_device,
+        head_per_device if one_head else on_device,
         mesh=mesh,
         in_specs=(
             P(("groups", "row"), "col"),

time: 405 us -> 95.5 us (0.24)
  the two profiles are of different devices: /device:TPU:0 before, /device:TPU:4 now
where the time goes in v1:
time: 95.5 us; the launch traced here: 95 us
  Pallas kernels  41.6 us (44%)
  starting transfers between devices  37.7 us (39%)
  local copies, waits for them, and re-layouts  6.19 us (6%)
  other arithmetic  4.79 us (5%)
  waiting for transfers between devices  3.92 us (4%)
    pallas_call x4, Pallas kernels, head_per_device(): pl.pallas_call(lambda *refs: attend_body(q_blocks, s == chunks - 1, *refs...  34.8 us
    ppermute x4, starting transfers between devices, head_per_device(): outs.append(lax.ppermute(og, axes, swap(q_perm(s))))  12.9 us
    ppermute x4, starting transfers between devices, head_per_device(): xs = [lax.ppermute(packed[s], axes, q_perm(s)) for s in range(chunks)]  8.89 us
    ppermute x4, starting transfers between devices, head_per_device(): tables = [lax.ppermute(table, axes, q_perm(s)) for s in range(chunks)]  8.46 us
    ppermute x3, starting transfers between devices, head_per_device(): lax.ppermute(packed[chunks + s], 'col', k_perm(s))  4.65 us
    pallas_call x2, Pallas kernels, unpack(): pl.pallas_call(unpack_body, out_shape=[whole, whole], in_specs=[SMEM] + [...  4.21 us
    unnamed x32, local copies, waits for them, and re-layouts  4.06 us
    ppermute x3, waiting for transfers between devices, head_per_device(): lax.ppermute(gkv[s], 'col', swap(k_perm(s)))  3.33 us
  transfers between devices with their start and end apart: 18, of which 2 were waited for; matrix products, arithmetic and copies ran while one was open for 7% of the time, Pallas kernels for 42%

profile of v1, /device:TPU:4, one launch (start us, length us, event | category | flops | bytes accessed | tf_op | source)
XLA Modules:
  0.0 95.0 jit_solution(16112763926258017328)
XLA Ops:
  0.7 0.6 copy-done.15
  1.3 0.1 copy.14
  1.4 0.1 pad_add_fusion
  1.5 0.7 collective-permute-start
  2.1 3.0 %collective-permute-start.6 = (s32[4,17]{1,0:T(4,128)S(1)}, s32[4,17]{1,0:T(4,128)S(1)}, u32[]{:S(2)}, u32[]{:S(2)}) collective-permute-start(s32[4,17]{1,0:T(4,128)S(1)} %pad_add_fusion), channel_id=1, source_target_pairs={{0,1},{1,5},{2,9},{3,13},{4,2},{5,6},{6,10},{7,14},{8,3},{9,7},{10... | collective-permute-start | bytes 824 | tf_op jit(solution)/shard_map/ppermute | solution.py:186
  5.1 3.5 %collective-permute-start.9 = (s32[4,17]{1,0:T(4,128)S(1)}, s32[4,17]{1,0:T(4,128)S(1)}, u32[]{:S(2)}, u32[]{:S(2)}) collective-permute-start(s32[4,17]{1,0:T(4,128)S(1)} %pad_add_fusion), channel_id=1, source_target_pairs={{0,2},{1,6},{2,10},{3,14},{4,3},{5,7},{6,11},{7,15},{8,0},{9,4},{1... | collective-permute-start | bytes 824 | tf_op jit(solution)/shard_map/ppermute | solution.py:186
  8.6 1.3 %collective-permute-start.12 = (s32[4,17]{1,0:T(4,128)S(1)}, s32[4,17]{1,0:T(4,128)S(1)}, u32[]{:S(2)}, u32[]{:S(2)}) collective-permute-start(s32[4,17]{1,0:T(4,128)S(1)} %pad_add_fusion), channel_id=1, source_target_pairs={{0,3},{1,7},{2,11},{3,15},{4,0},{5,4},{6,8},{7,12},{8,1},{9,5},{10... | collective-permute-start | bytes 824 | tf_op jit(solution)/shard_map/ppermute | solution.py:186
  9.9 0.7 pad_add_fusion.5.place
  10.6 2.6 %shard_map.93 = (bf16[512,128]{1,0:T(8,128)(2,1)}, bf16[512,128]{1,0:T(8,128)(2,1)}, bf16[512,128]{1,0:T(8,128)(2,1)}, bf16[512,128]{1,0:T(8,128)(2,1)}, bf16[51...) custom-call(s32[2]{0:T(128)} %pad_add_fusion.5.place, ...), custom_call_target="tpu_custom_call" | custom-call | tf_op jit(solution)/shard_map/pallas_call | solution.py:160
  13.2 1.6 %collective-permute-start.1 = (bf16[512,128]{1,0:T(8,128)(2,1)}, bf16[512,128]{1,0:T(8,128)(2,1)S(1)}, u32[]{:S(2)}, u32[]{:S(2)}) collective-permute-start(bf16[512,128]{1,0:T(8,128)(2,1)} %get-tuple-element.24), channel_id=1, source_target_pairs={{0,0},{1,4},{2,8},{3,12},{4,1},{5,5},{6,9},{7,13},{8,2},{9,6},{10,... | collective-permute-start | bytes 393224 | tf_op jit(solution)/shard_map/ppermute | solution.py:187
  14.7 0.0 collective-permute-done
  14.7 1.2 %collective-permute-start.2 = (bf16[512,128]{1,0:T(8,128)(2,1)}, bf16[512,128]{1,0:T(8,128)(2,1)S(1)}, u32[]{:S(2)}, u32[]{:S(2)}) collective-permute-start(bf16[512,128]{1,0:T(8,128)(2,1)} %get-tuple-element.26), channel_id=1, source_target_pairs={{0,1},{1,2},{2,3},{3,0},{4,5},{5,6},{6,7},{7,4},{8,9},{9,10},{10,1... | collective-permute-start | bytes 393224 | tf_op jit(solution)/shard_map/ppermute | solution.py:184
  16.0 0.0 collective-permute-done.6
  16.0 3.4 %collective-permute-start.3 = (bf16[512,128]{1,0:T(8,128)(2,1)}, bf16[512,128]{1,0:T(8,128)(2,1)S(1)}, u32[]{:S(2)}, u32[]{:S(2)}) collective-permute-start(bf16[512,128]{1,0:T(8,128)(2,1)} %get-tuple-element.27), channel_id=1, source_target_pairs={{0,2},{1,3},{2,0},{3,1},{4,6},{5,7},{6,4},{7,5},{8,10},{9,11},{10,... | collective-permute-start | bytes 393224 | tf_op jit(solution)/shard_map/ppermute | solution.py:184
  19.4 0.0 collective-permute-done.9
  19.4 0.1 collective-permute-start.4
  19.5 0.1 slice.41
  19.6 0.0 collective-permute-done.12
  19.6 0.5 collective-permute-start.7
  20.1 0.7 pad_add_fusion.1.refs_0_
  20.8 0.1 slice.43
  20.8 0.1 slice.45
  20.9 0.6 pad_add_fusion.2.refs_0_
  21.5 0.0 collective-permute-done.1.refs_1_
  21.5 6.8 %collective-permute-start.10 = (bf16[512,128]{1,0:T(8,128)(2,1)}, bf16[512,128]{1,0:T(8,128)(2,1)S(1)}, u32[]{:S(2)}, u32[]{:S(2)}) collective-permute-start(bf16[512,128]{1,0:T(8,128)(2,1)} %get-tuple-element.33), channel_id=1, source_target_pairs={{0,2},{1,6},{2,10},{3,14},{4,3},{5,7},{6,11},{7,15},{8,0},{9,4},{1... | collective-permute-start | bytes 393224 | tf_op jit(solution)/shard_map/ppermute | solution.py:187
  28.4 0.0 collective-permute-done.2.refs_3_
  28.4 0.0 collective-permute-start.13
  28.4 0.7 pad_add_fusion.3.refs_0_
  29.1 0.1 slice.47
  29.1 0.7 pad_add_fusion.4.refs_0_
  29.8 0.0 collective-permute-done.3.refs_4_
  29.8 0.0 collective-permute-done.4.refs_5_
  29.8 1.1 %broadcast_in_dim.7.refs_6_ = f32[2048,128]{1,0:T(8,128)} broadcast(f32[]{:T(128)} %constant.95.clone.1), dimensions={} | broadcast | bytes 1048580 | tf_op jit(solution)/shard_map/broadcast_in_dim | solution.py:189
  30.9 8.2 %shard_map.94 = (bf16[512,128]{1,0:T(8,128)(2,1)}, f32[2048,128]{1,0:T(8,128)}) custom-call(s32[4,17]{1,0:T(4,128)} %pad_add_fusion.1.refs_0_, bf16[512,128]{1,0:T(8,128)(2,1)} %copy-done.10, bf16[512,128]{1,0:T(8,128)(2,1)} %get-tuple-element.25.refs_2_, bf16[512,128]{1,0:T(8,128)(2,1)} %copy-done, ...), custom_call_target="tpu_custom_call", output_to_operand_aliasing={{1}: (6, {})} | custom-call | tf_op jit(solution)/shard_map/pallas_call | solution.py:197
  39.1 1.6 %collective-permute-start.5 = (bf16[512,128]{1,0:T(8,128)(2,1)}, bf16[512,128]{1,0:T(8,128)(2,1)S(1)}, u32[]{:S(2)}, u32[]{:S(2)}) collective-permute-start(bf16[512,128]{1,0:T(8,128)(2,1)} %get-tuple-element.29), channel_id=1, source_target_pairs={{0,0},{4,1},{8,2},{12,3},{1,4},{5,5},{9,6},{13,7},{2,8},{6,9},{10,... | collective-permute-start | bytes 393224 | tf_op jit(solution)/shard_map/ppermute | solution.py:209
  40.6 0.0 collective-permute-done.7.refs_1_
  40.6 0.7 copy-done.12
  41.3 5.9 %shard_map.95 = (bf16[512,128]{1,0:T(8,128)(2,1)}, f32[2048,128]{1,0:T(8,128)}) custom-call(s32[4,17]{1,0:T(4,128)} %pad_add_fusion.2.refs_0_, bf16[512,128]{1,0:T(8,128)(2,1)} %copy-done.12, bf16[512,128]{1,0:T(8,128)(2,1)} %get-tuple-element.25.refs_2_, bf16[512,128]{1,0:T(8,128)(2,1)} %copy-done, ...), custom_call_target="tpu_custom_call", output_to_operand_aliasing={{1}: (6, {})} | custom-call | tf_op jit(solution)/shard_map/pallas_call | solution.py:197
  47.2 4.8 %collective-permute-start.8 = (bf16[512,128]{1,0:T(8,128)(2,1)}, bf16[512,128]{1,0:T(8,128)(2,1)S(1)}, u32[]{:S(2)}, u32[]{:S(2)}) collective-permute-start(bf16[512,128]{1,0:T(8,128)(2,1)} %get-tuple-element.32), channel_id=1, source_target_pairs={{1,0},{5,1},{9,2},{13,3},{2,4},{6,5},{10,6},{14,7},{3,8},{7,9},{11... | collective-permute-start | bytes 393224 | tf_op jit(solution)/shard_map/ppermute | solution.py:209
  51.9 0.0 collective-permute-done.10.refs_1_
  51.9 0.7 copy-done.13
  52.6 11.3 %shard_map.96 = (bf16[512,128]{1,0:T(8,128)(2,1)}, f32[2048,128]{1,0:T(8,128)}) custom-call(s32[4,17]{1,0:T(4,128)} %pad_add_fusion.3.refs_0_, bf16[512,128]{1,0:T(8,128)(2,1)} %copy-done.13, bf16[512,128]{1,0:T(8,128)(2,1)} %get-tuple-element.25.refs_2_, bf16[512,128]{1,0:T(8,128)(2,1)} %copy-done, ...), custom_call_target="tpu_custom_call", output_to_operand_aliasing={{1}: (6, {})} | custom-call | tf_op jit(solution)/shard_map/pallas_call | solution.py:197
  63.9 6.6 %collective-permute-start.11 = (bf16[512,128]{1,0:T(8,128)(2,1)}, bf16[512,128]{1,0:T(8,128)(2,1)S(1)}, u32[]{:S(2)}, u32[]{:S(2)}) collective-permute-start(bf16[512,128]{1,0:T(8,128)(2,1)} %get-tuple-element.35), channel_id=1, source_target_pairs={{2,0},{6,1},{10,2},{14,3},{3,4},{7,5},{11,6},{15,7},{0,8},{4,9},{8... | collective-permute-start | bytes 393224 | tf_op jit(solution)/shard_map/ppermute | solution.py:209
  70.4 0.0 collective-permute-done.13.refs_1_
  70.4 0.7 copy-done.11
  71.1 9.5 %shard_map.97 = (bf16[512,128]{1,0:T(8,128)(2,1)}, f32[2048,128]{1,0:T(8,128)}) custom-call(s32[4,17]{1,0:T(4,128)} %pad_add_fusion.4.refs_0_, bf16[512,128]{1,0:T(8,128)(2,1)} %copy-done.11, bf16[512,128]{1,0:T(8,128)(2,1)} %get-tuple-element.25.refs_2_, bf16[512,128]{1,0:T(8,128)(2,1)} %copy-done, ...), custom_call_target="tpu_custom_call", output_to_operand_aliasing={{1}: (6, {})} | custom-call | tf_op jit(solution)/shard_map/pallas_call | solution.py:197
  80.6 0.0 collective-permute-start.14
  80.6 1.3 %fusion = bf16[2048,128]{1,0:T(8,128)(2,1)S(1)} fusion(f32[2048,128]{1,0:T(8,128)} %get-tuple-element.41, pred[128]{0:T(512)(128)(4,1)S(1)} %iota_compare_fusion), kind=kLoop, calls=%fused_computation.1 | loop fusion | flops 786432 | bytes 1572992 | tf_op jit(solution)/shard_map/convert_element_type | solution.py:149
  81.9 0.7 fusion.21
  82.6 1.7 %collective-permute-start.15 = (bf16[512,128]{1,0:T(8,128)(2,1)S(1)}, bf16[512,128]{1,0:T(8,128)(2,1)S(1)}, u32[]{:S(2)}, u32[]{:S(2)}) collective-permute-start(bf16[512,128]{1,0:T(8,128)(2,1)S(1)} %get-tuple-element.46), channel_id=1, source_target_pairs={{1,0},{2,1},{3,2},{0,3},{5,4},{6,5},{7,6},{4,7},{9,8},{10,9},{11,1... | collective-permute-start | bytes 393224 | tf_op jit(solution)/shard_map/ppermute | solution.py:211
  84.3 0.0 collective-permute-done.5.refs_0_
  84.4 0.9 collective-permute-start.16
  85.3 0.0 collective-permute-done.8.refs_1_
  85.3 0.2 collective-permute-start.17
  85.5 0.0 collective-permute-done.11.refs_2_
  85.5 0.6 collective-permute-done.14.refs_3_
  86.0 0.1 copy-done.5
  86.1 0.6 copy-done.7
  86.8 2.1 %shard_map.98 = (bf16[512,256]{1,0:T(8,128)(2,1)}, bf16[512,256]{1,0:T(8,128)(2,1)}) custom-call(s32[1]{0:T(128)} %bitcast.place, bf16[512,128]{1,0:T(8,128)(2,1)} %copy-done.3, bf16[512,128]{1,0:T(8,128)(2,1)} %copy-done.4, bf16[512,128]{1,0:T(8,128)(2,1)} %copy-done.5, bf16[512,128]{1,0:T(8,128)(2,1)} %copy-done.7), custom_call_target="tpu_custom_call" | custom-call | tf_op jit(solution)/shard_map/pallas_call | solution.py:216
  88.9 0.0 collective-permute-done.15.refs_1_
  88.9 3.3 %collective-permute-done.16.refs_2_ = bf16[512,128]{1,0:T(8,128)(2,1)S(1)} collective-permute-done((bf16[512,128]{1,0:T(8,128)(2,1)S(1)}, bf16[512,128]{1,0:T(8,128)(2,1)S(1)}, u32[]{:S(2)}, u32[]{:S(2)}) %collective-permute-start.16) | collective-permute-done | bytes 131104 | tf_op jit(solution)/shard_map/ppermute | solution.py:211
  92.2 0.6 copy-done.8
  92.9 0.0 copy-done.9
  92.9 2.1 %shard_map.99 = (bf16[512,256]{1,0:T(8,128)(2,1)}, bf16[512,256]{1,0:T(8,128)(2,1)}) custom-call(s32[1]{0:T(128)} %bitcast.2.place, bf16[512,128]{1,0:T(8,128)(2,1)} %get-tuple-element.47.refs_0_, bf16[512,128]{1,0:T(8,128)(2,1)} %copy-done.6, bf16[512,128]{1,0:T(8,128)(2,1)} %copy-done.8, bf16[512,128]{1,0:T(8,128)(2,1)} %copy-done.9), custom_call_target="tpu_custom_call" | custom-call | tf_op jit(solution)/shard_map/pallas_call | solution.py:216
  (30 shorter events, 0.1 us)
Async XLA Ops:
  0.6 0.7 copy-start.15
  0.6 0.7 copy-start.14
  1.5 13.3 %collective-permute-start = (s32[4,17]{1,0:T(4,128)S(1)}, s32[4,17]{1,0:T(4,128)S(1)}, u32[]{:S(2)}, u32[]{:S(2)}) collective-permute-start(s32[4,17]{1,0:T(4,128)S(1)} %pad_add_fusion), channel_id=1, source_target_pairs={{0,0},{1,4},{2,8},{3,12},{4,1},{5,5},{6,9},{7,13},{8,2},{9,6},{10,... | collective-permute-start | bytes 824 | tf_op jit(solution)/shard_map/ppermute | solution.py:186
  2.1 13.9 %collective-permute-start.6 = (s32[4,17]{1,0:T(4,128)S(1)}, s32[4,17]{1,0:T(4,128)S(1)}, u32[]{:S(2)}, u32[]{:S(2)}) collective-permute-start(s32[4,17]{1,0:T(4,128)S(1)} %pad_add_fusion), channel_id=1, source_target_pairs={{0,1},{1,5},{2,9},{3,13},{4,2},{5,6},{6,10},{7,14},{8,3},{9,7},{10... | collective-permute-start | bytes 824 | tf_op jit(solution)/shard_map/ppermute | solution.py:186
  5.1 14.3 %collective-permute-start.9 = (s32[4,17]{1,0:T(4,128)S(1)}, s32[4,17]{1,0:T(4,128)S(1)}, u32[]{:S(2)}, u32[]{:S(2)}) collective-permute-start(s32[4,17]{1,0:T(4,128)S(1)} %pad_add_fusion), channel_id=1, source_target_pairs={{0,2},{1,6},{2,10},{3,14},{4,3},{5,7},{6,11},{7,15},{8,0},{9,4},{1... | collective-permute-start | bytes 824 | tf_op jit(solution)/shard_map/ppermute | solution.py:186
  8.6 11.0 %collective-permute-start.12 = (s32[4,17]{1,0:T(4,128)S(1)}, s32[4,17]{1,0:T(4,128)S(1)}, u32[]{:S(2)}, u32[]{:S(2)}) collective-permute-start(s32[4,17]{1,0:T(4,128)S(1)} %pad_add_fusion), channel_id=1, source_target_pairs={{0,3},{1,7},{2,11},{3,15},{4,0},{5,4},{6,8},{7,12},{8,1},{9,5},{10... | collective-permute-start | bytes 824 | tf_op jit(solution)/shard_map/ppermute | solution.py:186
  13.2 8.4 %collective-permute-start.1 = (bf16[512,128]{1,0:T(8,128)(2,1)}, bf16[512,128]{1,0:T(8,128)(2,1)S(1)}, u32[]{:S(2)}, u32[]{:S(2)}) collective-permute-start(bf16[512,128]{1,0:T(8,128)(2,1)} %get-tuple-element.24), channel_id=1, source_target_pairs={{0,0},{1,4},{2,8},{3,12},{4,1},{5,5},{6,9},{7,13},{8,2},{9,6},{10,... | collective-permute-start | bytes 393224 | tf_op jit(solution)/shard_map/ppermute | solution.py:187
  14.7 13.6 %collective-permute-start.2 = (bf16[512,128]{1,0:T(8,128)(2,1)}, bf16[512,128]{1,0:T(8,128)(2,1)S(1)}, u32[]{:S(2)}, u32[]{:S(2)}) collective-permute-start(bf16[512,128]{1,0:T(8,128)(2,1)} %get-tuple-element.26), channel_id=1, source_target_pairs={{0,1},{1,2},{2,3},{3,0},{4,5},{5,6},{6,7},{7,4},{8,9},{9,10},{10,1... | collective-permute-start | bytes 393224 | tf_op jit(solution)/shard_map/ppermute | solution.py:184
  16.0 13.8 %collective-permute-start.3 = (bf16[512,128]{1,0:T(8,128)(2,1)}, bf16[512,128]{1,0:T(8,128)(2,1)S(1)}, u32[]{:S(2)}, u32[]{:S(2)}) collective-permute-start(bf16[512,128]{1,0:T(8,128)(2,1)} %get-tuple-element.27), channel_id=1, source_target_pairs={{0,2},{1,3},{2,0},{3,1},{4,6},{5,7},{6,4},{7,5},{8,10},{9,11},{10,... | collective-permute-start | bytes 393224 | tf_op jit(solution)/shard_map/ppermute | solution.py:184
  19.4 10.4 %collective-permute-start.4 = (bf16[512,128]{1,0:T(8,128)(2,1)}, bf16[512,128]{1,0:T(8,128)(2,1)S(1)}, u32[]{:S(2)}, u32[]{:S(2)}) collective-permute-start(bf16[512,128]{1,0:T(8,128)(2,1)} %get-tuple-element.28), channel_id=1, source_target_pairs={{0,3},{1,0},{2,1},{3,2},{4,7},{5,4},{6,5},{7,6},{8,11},{9,8},{10,9... | collective-permute-start | bytes 393224 | tf_op jit(solution)/shard_map/ppermute | solution.py:184
  19.6 21.1 %collective-permute-start.7 = (bf16[512,128]{1,0:T(8,128)(2,1)}, bf16[512,128]{1,0:T(8,128)(2,1)S(1)}, u32[]{:S(2)}, u32[]{:S(2)}) collective-permute-start(bf16[512,128]{1,0:T(8,128)(2,1)} %get-tuple-element.30), channel_id=1, source_target_pairs={{0,1},{1,5},{2,9},{3,13},{4,2},{5,6},{6,10},{7,14},{8,3},{9,7},{10... | collective-permute-start | bytes 393224 | tf_op jit(solution)/shard_map/ppermute | solution.py:187
  21.5 9.3 %copy-start.10 = (bf16[512,128]{1,0:T(8,128)(2,1)}, bf16[512,128]{1,0:T(8,128)(2,1)S(1)}, u32[]{:S(2)}) copy-start(bf16[512,128]{1,0:T(8,128)(2,1)S(1)} %collective-permute-done.1.refs_1_) | copy-start | bytes 393220
  21.5 30.4 %collective-permute-start.10 = (bf16[512,128]{1,0:T(8,128)(2,1)}, bf16[512,128]{1,0:T(8,128)(2,1)S(1)}, u32[]{:S(2)}, u32[]{:S(2)}) collective-permute-start(bf16[512,128]{1,0:T(8,128)(2,1)} %get-tuple-element.33), channel_id=1, source_target_pairs={{0,2},{1,6},{2,10},{3,14},{4,3},{5,7},{6,11},{7,15},{8,0},{9,4},{1... | collective-permute-start | bytes 393224 | tf_op jit(solution)/shard_map/ppermute | solution.py:187
  28.4 2.5 %copy-start = (bf16[512,128]{1,0:T(8,128)(2,1)}, bf16[512,128]{1,0:T(8,128)(2,1)S(1)}, u32[]{:S(2)}) copy-start(bf16[512,128]{1,0:T(8,128)(2,1)S(1)} %collective-permute-done.2.refs_3_) | copy-start | bytes 393220
  28.4 42.0 %collective-permute-start.13 = (bf16[512,128]{1,0:T(8,128)(2,1)}, bf16[512,128]{1,0:T(8,128)(2,1)S(1)}, u32[]{:S(2)}, u32[]{:S(2)}) collective-permute-start(bf16[512,128]{1,0:T(8,128)(2,1)} %get-tuple-element.36), channel_id=1, source_target_pairs={{0,3},{1,7},{2,11},{3,15},{4,0},{5,4},{6,8},{7,12},{8,1},{9,5},{10... | collective-permute-start | bytes 393224 | tf_op jit(solution)/shard_map/ppermute | solution.py:187
  29.8 1.1 %copy-start.1 = (bf16[512,128]{1,0:T(8,128)(2,1)}, bf16[512,128]{1,0:T(8,128)(2,1)S(1)}, u32[]{:S(2)}) copy-start(bf16[512,128]{1,0:T(8,128)(2,1)S(1)} %collective-permute-done.3.refs_4_) | copy-start | bytes 393220
  29.8 1.1 %copy-start.2 = (bf16[512,128]{1,0:T(8,128)(2,1)}, bf16[512,128]{1,0:T(8,128)(2,1)S(1)}, u32[]{:S(2)}) copy-start(bf16[512,128]{1,0:T(8,128)(2,1)S(1)} %collective-permute-done.4.refs_5_) | copy-start | bytes 393220
  39.1 45.3 %collective-permute-start.5 = (bf16[512,128]{1,0:T(8,128)(2,1)}, bf16[512,128]{1,0:T(8,128)(2,1)S(1)}, u32[]{:S(2)}, u32[]{:S(2)}) collective-permute-start(bf16[512,128]{1,0:T(8,128)(2,1)} %get-tuple-element.29), channel_id=1, source_target_pairs={{0,0},{4,1},{8,2},{12,3},{1,4},{5,5},{9,6},{13,7},{2,8},{6,9},{10,... | collective-permute-start | bytes 393224 | tf_op jit(solution)/shard_map/ppermute | solution.py:209
  40.6 0.7 copy-start.12
  47.2 38.1 %collective-permute-start.8 = (bf16[512,128]{1,0:T(8,128)(2,1)}, bf16[512,128]{1,0:T(8,128)(2,1)S(1)}, u32[]{:S(2)}, u32[]{:S(2)}) collective-permute-start(bf16[512,128]{1,0:T(8,128)(2,1)} %get-tuple-element.32), channel_id=1, source_target_pairs={{1,0},{5,1},{9,2},{13,3},{2,4},{6,5},{10,6},{14,7},{3,8},{7,9},{11... | collective-permute-start | bytes 393224 | tf_op jit(solution)/shard_map/ppermute | solution.py:209
  51.9 0.7 copy-start.13
  63.9 21.6 %collective-permute-start.11 = (bf16[512,128]{1,0:T(8,128)(2,1)}, bf16[512,128]{1,0:T(8,128)(2,1)S(1)}, u32[]{:S(2)}, u32[]{:S(2)}) collective-permute-start(bf16[512,128]{1,0:T(8,128)(2,1)} %get-tuple-element.35), channel_id=1, source_target_pairs={{2,0},{6,1},{10,2},{14,3},{3,4},{7,5},{11,6},{15,7},{0,8},{4,9},{8... | collective-permute-start | bytes 393224 | tf_op jit(solution)/shard_map/ppermute | solution.py:209
  70.4 0.7 copy-start.11
  80.6 5.4 %collective-permute-start.14 = (bf16[512,128]{1,0:T(8,128)(2,1)}, bf16[512,128]{1,0:T(8,128)(2,1)S(1)}, u32[]{:S(2)}, u32[]{:S(2)}) collective-permute-start(bf16[512,128]{1,0:T(8,128)(2,1)} %get-tuple-element.38), channel_id=1, source_target_pairs={{3,0},{7,1},{11,2},{15,3},{0,4},{4,5},{8,6},{12,7},{1,8},{5,9},{9,... | collective-permute-start | bytes 393224 | tf_op jit(solution)/shard_map/ppermute | solution.py:209
  82.6 6.3 %collective-permute-start.15 = (bf16[512,128]{1,0:T(8,128)(2,1)S(1)}, bf16[512,128]{1,0:T(8,128)(2,1)S(1)}, u32[]{:S(2)}, u32[]{:S(2)}) collective-permute-start(bf16[512,128]{1,0:T(8,128)(2,1)S(1)} %get-tuple-element.46), channel_id=1, source_target_pairs={{1,0},{2,1},{3,2},{0,3},{5,4},{6,5},{7,6},{4,7},{9,8},{10,9},{11,1... | collective-permute-start | bytes 393224 | tf_op jit(solution)/shard_map/ppermute | solution.py:211
  84.4 1.7 %copy-start.3 = (bf16[512,128]{1,0:T(8,128)(2,1)}, bf16[512,128]{1,0:T(8,128)(2,1)S(1)}, u32[]{:S(2)}) copy-start(bf16[512,128]{1,0:T(8,128)(2,1)S(1)} %collective-permute-done.5.refs_0_) | copy-start | bytes 393220
  84.4 7.8 %collective-permute-start.16 = (bf16[512,128]{1,0:T(8,128)(2,1)S(1)}, bf16[512,128]{1,0:T(8,128)(2,1)S(1)}, u32[]{:S(2)}, u32[]{:S(2)}) collective-permute-start(bf16[512,128]{1,0:T(8,128)(2,1)S(1)} %get-tuple-element.45), channel_id=1, source_target_pairs={{2,0},{3,1},{0,2},{1,3},{6,4},{7,5},{4,6},{5,7},{10,8},{11,9},{8,1... | collective-permute-start | bytes 393224 | tf_op jit(solution)/shard_map/ppermute | solution.py:211
  85.3 0.7 copy-start.4
  85.3 6.9 %collective-permute-start.17 = (bf16[512,128]{1,0:T(8,128)(2,1)S(1)}, bf16[512,128]{1,0:T(8,128)(2,1)S(1)}, u32[]{:S(2)}, u32[]{:S(2)}) collective-permute-start(bf16[512,128]{1,0:T(8,128)(2,1)S(1)} %get-tuple-element.44), channel_id=1, source_target_pairs={{3,0},{0,1},{1,2},{2,3},{7,4},{4,5},{5,6},{6,7},{11,8},{8,9},{9,10... | collective-permute-start | bytes 393224 | tf_op jit(solution)/shard_map/ppermute | solution.py:211
  85.5 0.7 copy-start.5
  86.1 0.7 copy-start.7
  88.9 3.3 %copy-start.6 = (bf16[512,128]{1,0:T(8,128)(2,1)}, bf16[512,128]{1,0:T(8,128)(2,1)S(1)}, u32[]{:S(2)}) copy-start(bf16[512,128]{1,0:T(8,128)(2,1)S(1)} %collective-permute-done.15.refs_1_) | copy-start | bytes 393220
  92.2 0.7 copy-start.8
  92.2 0.7 copy-start.9

commit v2 on v0

--- a/solution.py
+++ b/solution.py
@@ -1,8 +1,11 @@
+import functools
 import math
 
 import jax
 import jax.numpy as jnp
 from jax import lax
+from jax.experimental import pallas as pl
+from jax.experimental.pallas import tpu as pltpu
 from jax.sharding import PartitionSpec as P
 
 D = 1024
@@ -13,6 +16,318 @@
 
 
 NEG_FILL = -1e30
+GROUP = 4
+STREAMS = 4
+TAIL = 16
+VMEM = pl.BlockSpec(memory_space=pltpu.VMEM)
+SMEM = pl.BlockSpec(memory_space=pltpu.SMEM)
+
+
+def pack_body(place, lists, counts, q_ref, g_ref, k_ref, v_ref, *outs):
+    chunks = q_ref.shape[1] // HEAD
+    rows = q_ref.shape[0]
+
+    def pack(left_ref, right_ref, out_refs, at):
+        for step in range(chunks):
+            head = (at + step) % chunks
+            lanes = slice(head * HEAD, (head + 1) * HEAD)
+            out_refs[step][:rows, :] = jnp.concatenate(
+                [left_ref[:, lanes], right_ref[:, lanes]], axis=1
+            )
+
+    for at in range(chunks):
+
+        @pl.when(place[1] == at)
+        def _():
+            pack(k_ref, v_ref, outs[chunks:], at)
+
+        @pl.when(place[0] == at)
+        def _():
+            pack(q_ref, g_ref, outs[:chunks], at)
+
+    row = lax.broadcasted_iota(jnp.int32, (TAIL, 2 * HEAD), 0)
+    lane = lax.broadcasted_iota(jnp.int32, (TAIL, 2 * HEAD), 1)
+    table = jnp.zeros((TAIL, 2 * HEAD), jnp.int32)
+    for qb in range(rows // BLK):
+        line = jnp.where(lane == MAXNB, counts[qb], 0)
+        for at in range(MAXNB):
+            line = jnp.where(lane == at, lists[qb, at], line)
+        table = jnp.where(row == qb, line, table)
+    table = table.astype(jnp.float32).astype(jnp.bfloat16)
+    for out_ref in outs[:chunks]:
+        out_ref[rows:, :] = table
+
+
+def unpack_body(place, *refs):
+    left_ref, right_ref = refs[-2:]
+    chunks = len(refs) - 2
+    for at in range(chunks):
+
+        @pl.when(place[0] == at)
+        def _():
+            parts = [refs[(head - at) % chunks][...] for head in range(chunks)]
+            left_ref[...] = jnp.concatenate([p[:, :HEAD] for p in parts], axis=1)
+            right_ref[...] = jnp.concatenate([p[:, HEAD:] for p in parts], axis=1)
+
+
+def fold(x, op):
+    return op(x.reshape(x.shape[0] // 8, 8, x.shape[1]), axis=0)
+
+
+def attend_body(chunks, place, *refs):
+    x_refs, kv_refs = refs[:chunks], refs[chunks : 2 * chunks]
+    og_refs, gkv_refs = refs[2 * chunks : 3 * chunks], refs[3 * chunks : 4 * chunks]
+    (x_all, kv_all, wide, table, items, both, both_t, kv_t, stat, tiles, tops) = refs[
+        4 * chunks : 4 * chunks + 11
+    ]
+    rest = refs[4 * chunks + 11 :]
+    sem, table_sem = rest[:2]
+    rest = rest[2:]
+    accs, outs, stats = rest[:STREAMS], rest[STREAMS : 2 * STREAMS], rest[2 * STREAMS :]
+    scale = 1.0 / math.sqrt(HEAD)
+    to_log2 = scale * math.log2(math.e)
+    rows = kv_refs[0].shape[0]
+    per_chunk = rows // BLK
+    blocks = chunks * per_chunk
+
+    copies = []
+    for c in range(chunks):
+        copies.append(pltpu.make_async_copy(x_refs[c], x_all.at[c], sem.at[c]))
+        copies.append(
+            pltpu.make_async_copy(
+                kv_refs[c], kv_all.at[pl.ds(c * rows, rows), :], sem.at[chunks + c]
+            )
+        )
+    for copy in copies:
+        copy.start()
+    for s in range(STREAMS):
+        accs[s][...] = jnp.zeros_like(accs[s])
+        outs[s][...] = jnp.zeros_like(outs[s])
+        stats[s][0] = jnp.full(stats[s].shape[1:], NEG_FILL, jnp.float32)
+        stats[s][1] = jnp.zeros(stats[s].shape[1:], jnp.float32)
+        stats[s][2] = jnp.zeros(stats[s].shape[1:], jnp.float32)
+    for copy in copies:
+        copy.wait()
+
+    lane = lax.broadcasted_iota(jnp.int32, (TAIL, 2 * HEAD), 1)
+    for c in range(chunks):
+        listed = x_all[c, rows:, :].astype(jnp.float32).astype(jnp.int32)
+        part = lax.rem(place[1] - lax.div(listed, per_chunk) + chunks, chunks)
+        slot = part * per_chunk + lax.rem(listed, per_chunk)
+        wide[c * TAIL : (c + 1) * TAIL, :] = jnp.where(lane < MAXNB, slot, listed)
+    copy = pltpu.make_async_copy(wide, table, table_sem)
+    copy.start()
+
+    is_left = lax.broadcasted_iota(jnp.int32, (BLK, 2 * HEAD), 1) < HEAD
+    zeros = jnp.zeros((HEAD, BLK), jnp.bfloat16)
+    for b in range(blocks):
+        kv_t[:, b * BLK : (b + 1) * BLK] = kv_all[b * BLK : (b + 1) * BLK, :].T
+        at = (b % per_chunk) * BLK
+        x = x_all[b // per_chunk, at : at + BLK, :]
+        both[b, :BLK, :] = jnp.where(is_left, x, jnp.zeros_like(x))
+        both[b, BLK:, :] = jnp.where(is_left, jnp.zeros_like(x), x)
+        x_t = x.T
+        both_t[b, :HEAD, :BLK] = x_t[:HEAD]
+        both_t[b, :HEAD, BLK:] = zeros
+        both_t[b, HEAD:, :BLK] = zeros
+        both_t[b, HEAD:, BLK:] = x_t[HEAD:]
+    copy.wait()
+
+    def line(qb):
+        return lax.div(qb, per_chunk) * TAIL + lax.rem(qb, per_chunk)
+
+    def add_items(qb, count):
+        groups = (table[line(qb), MAXNB] + GROUP - 1) // GROUP
+
+        def add_item(g, _):
+            items[0, count + g] = qb
+            items[1, count + g] = g * GROUP
+            return 0
+
+        lax.fori_loop(0, groups, add_item, 0)
+        return count + groups
+
+    count = lax.fori_loop(0, blocks, add_items, 0)
+    steps = (count + STREAMS - 1) // STREAMS
+    for s in range(STREAMS - 1):
+        items[0, count + s] = 0
+        items[1, count + s] = MAXNB
+
+    def item(at):
+        qb, base = items[0, at], items[1, at]
+        slots = [
+            pl.multiple_of(table[line(qb), jnp.minimum(base + u, MAXNB - 1)] * BLK, BLK)
+            for u in range(GROUP)
+        ]
+        return qb, base, slots
+
+    def score_step(i, _):
+        for s in range(STREAMS):
+            at = s * steps + i
+            qb, base, slots = item(at)
+            live = table[line(qb), MAXNB]
+            kv = jnp.concatenate([kv_all[pl.ds(k, BLK), :] for k in slots], axis=0)
+            both_scores = jnp.dot(kv, both_t[qb], preferred_element_type=jnp.float32)
+            scores = [
+                both_scores[u * BLK : (u + 1) * BLK, :BLK] * to_log2
+                + jnp.where(base + u < live, 0.0, NEG_FILL)
+                for u in range(GROUP)
+            ]
+            top = functools.reduce(jnp.maximum, [fold(v, jnp.max) for v in scores])
+            top = jnp.max(top, axis=0, keepdims=True)
+            total = jnp.zeros((8, BLK), jnp.float32)
+            dot = jnp.zeros((8, BLK), jnp.float32)
+            for u in range(GROUP):
+                part = slice(u * BLK, (u + 1) * BLK)
+                e = jnp.exp2(scores[u] - top)
+                dw = both_scores[part, BLK:]
+                tiles[at, part, :BLK] = e
+                tiles[at, part, BLK:] = dw
+                total = total + fold(e, jnp.sum)
+                dot = dot + fold(e * dw, jnp.sum)
+            total = jnp.sum(total, axis=0, keepdims=True)
+            dot = jnp.sum(dot, axis=0, keepdims=True)
+            tops[pl.ds(at, 1), :] = top
+            row = pl.ds(qb, 1)
+            old = stats[s][0, row, :]
+            new = jnp.maximum(old, top)
+            old_part, new_part = jnp.exp2(old - new), jnp.exp2(top - new)
+            stats[s][0, row, :] = new
+            stats[s][1, row, :] = stats[s][1, row, :] * old_part + total * new_part
+            stats[s][2, row, :] = stats[s][2, row, :] * old_part + dot * new_part
+        return 0
+
+    lax.fori_loop(0, steps, score_step, 0)
+
+    top = functools.reduce(jnp.maximum, [st[0] for st in stats])
+    total = functools.reduce(jnp.add, [st[1] * jnp.exp2(st[0] - top) for st in stats])
+    dot = functools.reduce(jnp.add, [st[2] * jnp.exp2(st[0] - top) for st in stats])
+    stat[0] = top
+    stat[1] = 1.0 / total
+    stat[2] = dot / total
+
+    def grad_step(i, _):
+        for s in range(STREAMS):
+            at = s * steps + i
+            qb, base, slots = item(at)
+            row = pl.ds(qb, 1)
+            factor = stat[1, row, :] * jnp.exp2(tops[pl.ds(at, 1), :] - stat[0, row, :])
+            delta = stat[2, row, :]
+            w, ds = [], []
+            for u in range(GROUP):
+                part = slice(u * BLK, (u + 1) * BLK)
+                weights = tiles[at, part, :BLK] * factor
+                ds.append((weights * (tiles[at, part, BLK:] - delta)).astype(jnp.bfloat16))
+                w.append(weights.astype(jnp.bfloat16))
+            pair = jnp.concatenate(
+                [jnp.concatenate(ds, axis=0), jnp.concatenate(w, axis=0)], axis=1
+            )
+            grads = jnp.dot(pair, both[qb], preferred_element_type=jnp.float32)
+            for u in range(GROUP):
+                accs[s][pl.ds(slots[u], BLK), :] += grads[u * BLK : (u + 1) * BLK]
+            t = jnp.concatenate([kv_t[:, pl.ds(k, BLK)] for k in slots], axis=1)
+            sums = jnp.dot(t, pair, preferred_element_type=jnp.float32)
+            outs[s][qb, :HEAD, :] += sums[HEAD:, BLK:]
+            outs[s][qb, HEAD:, :] += sums[:HEAD, :BLK]
+        return 0
+
+    lax.fori_loop(0, steps, grad_step, 0)
+
+    is_out = lax.broadcasted_iota(jnp.int32, (2 * HEAD, BLK), 0) < HEAD
+    for b in range(blocks):
+        out = functools.reduce(jnp.add, [r[b] for r in outs])
+        out = jnp.where(is_out, out, out * scale)
+        at = (b % per_chunk) * BLK
+        og_refs[b // per_chunk][at : at + BLK, :] = out.T.astype(jnp.bfloat16)
+        acc = functools.reduce(jnp.add, [r[b * BLK : (b + 1) * BLK, :] for r in accs])
+        acc = jnp.where(is_left, acc * scale, acc)
+        gkv_refs[b // per_chunk][at : at + BLK, :] = acc.astype(jnp.bfloat16)
+
+
+def in_vmem(x):
+    return pltpu.with_memory_space_constraint(x, pltpu.VMEM)
+
+
+def head_per_device(queries, keys, values, cotangent, block_lists, block_counts):
+    chunks = 4
+    rows = queries.shape[0]
+    at_row, at_col = lax.axis_index("row"), lax.axis_index("col")
+    place = jnp.stack([at_row, at_col]).astype(jnp.int32)
+    chunk = pltpu.VMEM((rows, 2 * HEAD), jnp.bfloat16)
+    tailed = pltpu.VMEM((rows + TAIL, 2 * HEAD), jnp.bfloat16)
+    packed = pl.pallas_call(
+        pack_body,
+        out_shape=[tailed] * chunks + [chunk] * chunks,
+        in_specs=[SMEM] * 3 + [VMEM] * 4,
+        out_specs=[VMEM] * (2 * chunks),
+        name="pack",
+    )(place, block_lists, block_counts, queries, cotangent, keys, values)
+
+    def q_perm(step):
+        return [
+            (r * chunks + c, c * chunks + (r + step) % chunks)
+            for r in range(chunks)
+            for c in range(chunks)
+        ]
+
+    def k_perm(step):
+        return [(c, (c + step) % chunks) for c in range(chunks)]
+
+    def swap(perm):
+        return [(b, a) for a, b in perm]
+
+    axes = ("row", "col")
+    kv = [packed[chunks]] + [
+        lax.ppermute(packed[chunks + s], "col", k_perm(s)) for s in range(1, chunks)
+    ]
+    xs = [lax.ppermute(packed[s], axes, q_perm(s)) for s in range(chunks)]
+
+    blocks = chunks * rows // BLK
+    most = blocks * MAXNB // GROUP + STREAMS
+    results = pl.pallas_call(
+        functools.partial(attend_body, chunks),
+        out_shape=[chunk] * (2 * chunks),
+        in_specs=[SMEM] + [VMEM] * (2 * chunks),
+        out_specs=[VMEM] * (2 * chunks),
+        scratch_shapes=[
+            pltpu.VMEM((chunks, rows + TAIL, 2 * HEAD), jnp.bfloat16),
+            pltpu.VMEM((chunks * rows, 2 * HEAD), jnp.bfloat16),
+            pltpu.VMEM((chunks * TAIL, 2 * HEAD), jnp.int32),
+            pltpu.SMEM((chunks * TAIL, 2 * HEAD), jnp.int32),
+            pltpu.SMEM((2, most), jnp.int32),
+            pltpu.VMEM((blocks, 2 * BLK, 2 * HEAD), jnp.bfloat16),
+            pltpu.VMEM((blocks, 2 * HEAD, 2 * BLK), jnp.bfloat16),
+            pltpu.VMEM((2 * HEAD, chunks * rows), jnp.bfloat16),
+            pltpu.VMEM((3, blocks, BLK), jnp.float32),
+            pltpu.VMEM((most, GROUP * BLK, 2 * BLK), jnp.float32),
+            pltpu.VMEM((most, BLK), jnp.float32),
+            pltpu.SemaphoreType.DMA((2 * chunks,)),
+            pltpu.SemaphoreType.DMA,
+        ]
+        + [pltpu.VMEM((chunks * rows, 2 * HEAD), jnp.float32)] * STREAMS
+        + [pltpu.VMEM((blocks, 2 * HEAD, BLK), jnp.float32)] * STREAMS
+        + [pltpu.VMEM((3, blocks, BLK), jnp.float32)] * STREAMS,
+        compiler_params=pltpu.CompilerParams(vmem_limit_bytes=56 * 1024 * 1024),
+        name="attend",
+    )(place, *[in_vmem(a) for a in (*xs, *kv)])
+    ogs, gkv = results[:chunks], results[chunks:]
+    ogs = [lax.ppermute(ogs[s], axes, swap(q_perm(s))) for s in range(chunks)]
+    gkv = [gkv[0]] + [lax.ppermute(gkv[s], "col", swap(k_perm(s))) for s in range(1, chunks)]
+
+    whole = jax.ShapeDtypeStruct(queries.shape, jnp.bfloat16)
+
+    def unpack(at, parts):
+        return pl.pallas_call(
+            unpack_body,
+            out_shape=[whole, whole],
+            in_specs=[SMEM] + [VMEM] * chunks,
+            out_specs=[VMEM, VMEM],
+            name="unpack",
+        )(jnp.reshape(at, (1,)).astype(jnp.int32), *[in_vmem(p) for p in parts])
+
+    attended, grad_queries = unpack(at_row, ogs)
+    grad_keys, grad_values = unpack(at_col, gkv)
+    return attended, grad_queries, grad_keys, grad_values
 
 
 def tile_scores(query_tile, key_tile, score_scale):
@@ -190,8 +505,10 @@
 
 
 def solution(mesh):
+    rows, cols = mesh.shape["row"], mesh.shape["col"]
+    one_head = rows == 4 and cols == 4
     return jax.shard_map(
-        on_device,
+        head_per_device if one_head else on_device,
         mesh=mesh,
         in_specs=(
             P(("groups", "row"), "col"),

time: 405 us -> 72.5 us (0.18)
  waiting for transfers between devices: 224 us -> 21.6 us
  local copies, waits for them, and re-layouts: 54.1 us -> 0 us
  other arithmetic: 41 us -> 0.59 us
  matrix products: 40.2 us -> 0 us
  starting transfers between devices: 0.37 us -> 29.9 us
  blocking collectives: 20.9 us -> 0 us
  Pallas kernels: 0 us -> 18.9 us
  between operations: 14 us -> 0.69 us
  loops' own time: 8.26 us -> 0 us
    reduce_scatter x4 -> x0, waiting for transfers between devices: 142 us -> none  [the longest x1 44.5 us: on_device(): lax.psum_scatter(key_parts, 'row', scatter_dimension=1, tiled=True)]
    all_gather x5 -> x0, waiting for transfers between devices: 82.2 us -> none  [the longest x1 30.1 us: on_device(): lax.all_gather(keys, 'row', axis=1, tiled=True)]
    dot_general x28 -> x0, matrix products: 40.2 us -> none  [the longest x4 15.3 us: output_work(): jnp.einsum('hqk,khd->qhd', weights, value_heads, preferred_element_type=j...]
    ppermute x0 -> x14, starting transfers between devices: none -> 29.9 us  [the longest x4 11.4 us: head_per_device(): ogs = [lax.ppermute(ogs[s], axes, swap(q_perm(s))) for s in range(chunks)]]
    ppermute x0 -> x14, waiting for transfers between devices: none -> 21.6 us  [the longest x4 10.5 us: head_per_device(): xs = [lax.ppermute(packed[s], axes, q_perm(s)) for s in range(chunks)]]
    dynamic_slice x28 -> x0, local copies, waits for them, and re-layouts: 19.1 us -> none  [the longest x8 11 us: tile_parts(): value_tile = lax.dynamic_slice_in_dim(v_full, key_at * BLK, BLK, 0)]
    pallas_call x0 -> x4, Pallas kernels: none -> 18.9 us  [the longest x1 15.2 us: head_per_device(): pl.pallas_call(functools.partial(attend_body, chunks), out_shape=[chunk]...]
    convert_element_type x18 -> x0, other arithmetic: 14.5 us -> none  [the longest x4 2.6 us: output_step(): return lax.cond(tile_any[super_at, key_at], output_work, unchanged, carry)]
  transfers between devices with their start and end apart: 9 -> 14, of which waited for: 8 -> 4; matrix products, arithmetic and copies ran while one was open for 8% -> 0% of each run, Pallas kernels for 0% -> 1%
where the time goes in v2:
time: 72.5 us; the launch traced here: 71.7 us
  starting transfers between devices  29.9 us (41%)
  waiting for transfers between devices  21.6 us (30%)
  Pallas kernels  18.9 us (26%)
    pallas_call x1, Pallas kernels, head_per_device(): pl.pallas_call(functools.partial(attend_body, chunks), out_shape=[chunk]...  15.2 us
    ppermute x4, starting transfers between devices, head_per_device(): ogs = [lax.ppermute(ogs[s], axes, swap(q_perm(s))) for s in range(chunks)]  11.4 us
    ppermute x4, waiting for transfers between devices, head_per_device(): xs = [lax.ppermute(packed[s], axes, q_perm(s)) for s in range(chunks)]  10.5 us
    ppermute x3, waiting for transfers between devices, head_per_device(): lax.ppermute(packed[chunks + s], 'col', k_perm(s))  7.72 us
    ppermute x4, starting transfers between devices, head_per_device(): xs = [lax.ppermute(packed[s], axes, q_perm(s)) for s in range(chunks)]  7.63 us
    ppermute x3, starting transfers between devices, head_per_device(): lax.ppermute(gkv[s], 'col', swap(k_perm(s)))  7.33 us
    ppermute x3, starting transfers between devices, head_per_device(): lax.ppermute(packed[chunks + s], 'col', k_perm(s))  3.52 us
    ppermute x3, waiting for transfers between devices, head_per_device(): lax.ppermute(gkv[s], 'col', swap(k_perm(s)))  3.35 us
  transfers between devices with their start and end apart: 14, of which 4 were waited for; matrix products, arithmetic and copies ran while one was open for 0% of the time, Pallas kernels for 1%

profile of v2, /device:TPU:0, one launch (start us, length us, event | category | flops | bytes accessed | tf_op | source)
XLA Modules:
  0.0 71.7 jit_solution(16654258515999754982)
XLA Ops:
  0.6 0.6 pad_add_fusion.place
  1.2 1.7 %pack.1 = (bf16[528,128]{1,0:T(8,128)(2,1)S(1)}, bf16[528,128]{1,0:T(8,128)(2,1)S(1)}, bf16[528,128]{1,0:T(8,128)(2,1)S(1)}, bf16[528,128]{1,0:T(8,128)(2,1)S(1)...) custom-call(s32[2]{0:T(128)} %pad_add_fusion.place, ...), custom_call_target="tpu_custom_call" | custom-call | tf_op jit(solution)/shard_map/pack/pallas_call | solution.py:258
  2.9 0.5 collective-permute-start.4
  3.4 2.6 %collective-permute-start.5 = (bf16[512,128]{1,0:T(8,128)(2,1)S(1)}, bf16[512,128]{1,0:T(8,128)(2,1)S(1)}, u32[]{:S(2)}, u32[]{:S(2)}) collective-permute-start(bf16[512,128]{1,0:T(8,128)(2,1)S(1)} %get-tuple-element.30), channel_id=1, source_target_pairs={{0,2},{1,3},{2,0},{3,1},{4,6},{5,7},{6,4},{7,5},{8,10},{9,11},{10,... | collective-permute-start | bytes 393224 | tf_op jit(solution)/shard_map/ppermute | solution.py:281
  6.0 0.7 collective-permute-start
  6.6 3.0 %collective-permute-start.1 = (bf16[528,128]{1,0:T(8,128)(2,1)S(1)}, bf16[528,128]{1,0:T(8,128)(2,1)S(1)}, u32[]{:S(2)}, u32[]{:S(2)}) collective-permute-start(bf16[528,128]{1,0:T(8,128)(2,1)S(1)} %get-tuple-element.25), channel_id=1, source_target_pairs={{0,1},{1,5},{2,9},{3,13},{4,2},{5,6},{6,10},{7,14},{8,3},{9,7},{10... | collective-permute-start | bytes 405512 | tf_op jit(solution)/shard_map/ppermute | solution.py:283
  9.6 2.5 %collective-permute-start.2 = (bf16[528,128]{1,0:T(8,128)(2,1)S(1)}, bf16[528,128]{1,0:T(8,128)(2,1)S(1)}, u32[]{:S(2)}, u32[]{:S(2)}) collective-permute-start(bf16[528,128]{1,0:T(8,128)(2,1)S(1)} %get-tuple-element.26), channel_id=1, source_target_pairs={{0,2},{1,6},{2,10},{3,14},{4,3},{5,7},{6,11},{7,15},{8,0},{9,4},{1... | collective-permute-start | bytes 405512 | tf_op jit(solution)/shard_map/ppermute | solution.py:283
  12.1 0.0 collective-permute-done.4.refs_5_
  12.1 1.5 %collective-permute-start.3 = (bf16[528,128]{1,0:T(8,128)(2,1)S(1)}, bf16[528,128]{1,0:T(8,128)(2,1)S(1)}, u32[]{:S(2)}, u32[]{:S(2)}) collective-permute-start(bf16[528,128]{1,0:T(8,128)(2,1)S(1)} %get-tuple-element.27), channel_id=1, source_target_pairs={{0,3},{1,7},{2,11},{3,15},{4,0},{5,4},{6,8},{7,12},{8,1},{9,5},{10... | collective-permute-start | bytes 405512 | tf_op jit(solution)/shard_map/ppermute | solution.py:283
  13.6 0.0 collective-permute-done.5.refs_6_
  13.6 0.4 collective-permute-start.6
  14.1 7.7 %collective-permute-done.6.refs_7_ = bf16[512,128]{1,0:T(8,128)(2,1)S(1)} collective-permute-done((bf16[512,128]{1,0:T(8,128)(2,1)S(1)}, bf16[512,128]{1,0:T(8,128)(2,1)S(1)}, u32[]{:S(2)}, u32[]{:S(2)}) %collective-permute-start.6) | collective-permute-done | bytes 131104 | tf_op jit(solution)/shard_map/ppermute | solution.py:281
  21.8 0.0 collective-permute-done.refs_0_
  21.8 0.0 collective-permute-done.1.refs_1_
  21.8 10.5 %collective-permute-done.2.refs_2_ = bf16[528,128]{1,0:T(8,128)(2,1)S(1)} collective-permute-done((bf16[528,128]{1,0:T(8,128)(2,1)S(1)}, bf16[528,128]{1,0:T(8,128)(2,1)S(1)}, u32[]{:S(2)}, u32[]{:S(2)}) %collective-permute-start.2) | collective-permute-done | bytes 135200 | tf_op jit(solution)/shard_map/ppermute | solution.py:283
  32.3 0.0 collective-permute-done.3.refs_3_
  32.3 15.2 %attend.1 = (bf16[512,128]{1,0:T(8,128)(2,1)S(1)}, bf16[512,128]{1,0:T(8,128)(2,1)S(1)}, bf16[512,128]{1,0:T(8,128)(2,1)S(1)}, bf16[512,128]{1,0:T(8,128)(2,1)S(...) custom-call(s32[2]{0:T(128)} %pad_add_fusion.place, ...), custom_call_target="tpu_custom_call" | custom-call | tf_op jit(solution)/shard_map/attend/pallas_call | solution.py:287
  47.5 0.7 collective-permute-start.7
  48.2 7.9 %collective-permute-start.8 = (bf16[512,128]{1,0:T(8,128)(2,1)S(1)}, bf16[512,128]{1,0:T(8,128)(2,1)S(1)}, u32[]{:S(2)}, u32[]{:S(2)}) collective-permute-start(bf16[512,128]{1,0:T(8,128)(2,1)S(1)} %get-tuple-element.33), channel_id=1, source_target_pairs={{1,0},{5,1},{9,2},{13,3},{2,4},{6,5},{10,6},{14,7},{3,8},{7,9},{11... | collective-permute-start | bytes 393224 | tf_op jit(solution)/shard_map/ppermute | solution.py:314
  56.1 0.0 collective-permute-start.9
  56.1 2.8 %collective-permute-start.10 = (bf16[512,128]{1,0:T(8,128)(2,1)S(1)}, bf16[512,128]{1,0:T(8,128)(2,1)S(1)}, u32[]{:S(2)}, u32[]{:S(2)}) collective-permute-start(bf16[512,128]{1,0:T(8,128)(2,1)S(1)} %get-tuple-element.35), channel_id=1, source_target_pairs={{3,0},{7,1},{11,2},{15,3},{0,4},{4,5},{8,6},{12,7},{1,8},{5,9},{9,... | collective-permute-start | bytes 393224 | tf_op jit(solution)/shard_map/ppermute | solution.py:314
  58.9 0.0 collective-permute-start.11
  58.9 0.0 collective-permute-done.7.refs_0_
  58.9 7.3 %collective-permute-start.12 = (bf16[512,128]{1,0:T(8,128)(2,1)S(1)}, bf16[512,128]{1,0:T(8,128)(2,1)S(1)}, u32[]{:S(2)}, u32[]{:S(2)}) collective-permute-start(bf16[512,128]{1,0:T(8,128)(2,1)S(1)} %get-tuple-element.40), channel_id=1, source_target_pairs={{2,0},{3,1},{0,2},{1,3},{6,4},{7,5},{4,6},{5,7},{10,8},{11,9},{8,1... | collective-permute-start | bytes 393224 | tf_op jit(solution)/shard_map/ppermute | solution.py:315
  66.3 0.0 collective-permute-done.8.refs_1_
  66.3 0.0 collective-permute-start.13
  66.3 0.0 collective-permute-done.9.refs_2_
  66.3 0.0 collective-permute-done.10.refs_3_
  66.3 1.0 %unpack.2 = (bf16[512,256]{1,0:T(8,128)(2,1)}, bf16[512,256]{1,0:T(8,128)(2,1)}) custom-call(s32[1]{0:T(128)} %bitcast.place, bf16[512,128]{1,0:T(8,128)(2,1)S(1)} %collective-permute-done.7.refs_0_, bf16[512,128]{1,0:T(8,128)(2,1)S(1)} %collective-permute-done.8.refs_1_, bf16[512,128]{1,0:T(8,128)(2,1)S(1)} %collective-permute-done.9.refs_2_, ...), custom_call_target="tpu_custom_call" | custom-call | tf_op jit(solution)/shard_map/unpack/pallas_call | solution.py:320
  67.3 0.0 collective-permute-done.11.refs_1_
  67.3 2.8 %collective-permute-done.12.refs_2_ = bf16[512,128]{1,0:T(8,128)(2,1)S(1)} collective-permute-done((bf16[512,128]{1,0:T(8,128)(2,1)S(1)}, bf16[512,128]{1,0:T(8,128)(2,1)S(1)}, u32[]{:S(2)}, u32[]{:S(2)}) %collective-permute-start.12) | collective-permute-done | bytes 131104 | tf_op jit(solution)/shard_map/ppermute | solution.py:315
  70.1 0.6 collective-permute-done.13.refs_3_
  70.7 1.0 %unpack.3 = (bf16[512,256]{1,0:T(8,128)(2,1)}, bf16[512,256]{1,0:T(8,128)(2,1)}) custom-call(s32[1]{0:T(128)} %bitcast.1.place, bf16[512,128]{1,0:T(8,128)(2,1)S(1)} %get-tuple-element.38.refs_0_, bf16[512,128]{1,0:T(8,128)(2,1)S(1)} %collective-permute-done.11.refs_1_, bf16[512,128]{1,0:T(8,128)(2,1)S(1)} %collective-permute-done.12.refs_2_, ...), custom_call_target="tpu_custom_call" | custom-call | tf_op jit(solution)/shard_map/unpack/pallas_call | solution.py:320
Async XLA Ops:
  2.9 9.2 %collective-permute-start.4 = (bf16[512,128]{1,0:T(8,128)(2,1)S(1)}, bf16[512,128]{1,0:T(8,128)(2,1)S(1)}, u32[]{:S(2)}, u32[]{:S(2)}) collective-permute-start(bf16[512,128]{1,0:T(8,128)(2,1)S(1)} %get-tuple-element.29), channel_id=1, source_target_pairs={{0,1},{1,2},{2,3},{3,0},{4,5},{5,6},{6,7},{7,4},{8,9},{9,10},{10,1... | collective-permute-start | bytes 393224 | tf_op jit(solution)/shard_map/ppermute | solution.py:281
  3.4 10.2 %collective-permute-start.5 = (bf16[512,128]{1,0:T(8,128)(2,1)S(1)}, bf16[512,128]{1,0:T(8,128)(2,1)S(1)}, u32[]{:S(2)}, u32[]{:S(2)}) collective-permute-start(bf16[512,128]{1,0:T(8,128)(2,1)S(1)} %get-tuple-element.30), channel_id=1, source_target_pairs={{0,2},{1,3},{2,0},{3,1},{4,6},{5,7},{6,4},{7,5},{8,10},{9,11},{10,... | collective-permute-start | bytes 393224 | tf_op jit(solution)/shard_map/ppermute | solution.py:281
  6.0 15.8 %collective-permute-start = (bf16[528,128]{1,0:T(8,128)(2,1)S(1)}, bf16[528,128]{1,0:T(8,128)(2,1)S(1)}, u32[]{:S(2)}, u32[]{:S(2)}) collective-permute-start(bf16[528,128]{1,0:T(8,128)(2,1)S(1)} %get-tuple-element.24), channel_id=1, source_target_pairs={{0,0},{1,4},{2,8},{3,12},{4,1},{5,5},{6,9},{7,13},{8,2},{9,6},{10,... | collective-permute-start | bytes 405512 | tf_op jit(solution)/shard_map/ppermute | solution.py:283
  6.6 15.1 %collective-permute-start.1 = (bf16[528,128]{1,0:T(8,128)(2,1)S(1)}, bf16[528,128]{1,0:T(8,128)(2,1)S(1)}, u32[]{:S(2)}, u32[]{:S(2)}) collective-permute-start(bf16[528,128]{1,0:T(8,128)(2,1)S(1)} %get-tuple-element.25), channel_id=1, source_target_pairs={{0,1},{1,5},{2,9},{3,13},{4,2},{5,6},{6,10},{7,14},{8,3},{9,7},{10... | collective-permute-start | bytes 405512 | tf_op jit(solution)/shard_map/ppermute | solution.py:283
  9.6 22.6 %collective-permute-start.2 = (bf16[528,128]{1,0:T(8,128)(2,1)S(1)}, bf16[528,128]{1,0:T(8,128)(2,1)S(1)}, u32[]{:S(2)}, u32[]{:S(2)}) collective-permute-start(bf16[528,128]{1,0:T(8,128)(2,1)S(1)} %get-tuple-element.26), channel_id=1, source_target_pairs={{0,2},{1,6},{2,10},{3,14},{4,3},{5,7},{6,11},{7,15},{8,0},{9,4},{1... | collective-permute-start | bytes 405512 | tf_op jit(solution)/shard_map/ppermute | solution.py:283
  12.1 20.1 %collective-permute-start.3 = (bf16[528,128]{1,0:T(8,128)(2,1)S(1)}, bf16[528,128]{1,0:T(8,128)(2,1)S(1)}, u32[]{:S(2)}, u32[]{:S(2)}) collective-permute-start(bf16[528,128]{1,0:T(8,128)(2,1)S(1)} %get-tuple-element.27), channel_id=1, source_target_pairs={{0,3},{1,7},{2,11},{3,15},{4,0},{5,4},{6,8},{7,12},{8,1},{9,5},{10... | collective-permute-start | bytes 405512 | tf_op jit(solution)/shard_map/ppermute | solution.py:283
  13.6 8.2 %collective-permute-start.6 = (bf16[512,128]{1,0:T(8,128)(2,1)S(1)}, bf16[512,128]{1,0:T(8,128)(2,1)S(1)}, u32[]{:S(2)}, u32[]{:S(2)}) collective-permute-start(bf16[512,128]{1,0:T(8,128)(2,1)S(1)} %get-tuple-element.31), channel_id=1, source_target_pairs={{0,3},{1,0},{2,1},{3,2},{4,7},{5,4},{6,5},{7,6},{8,11},{9,8},{10,9... | collective-permute-start | bytes 393224 | tf_op jit(solution)/shard_map/ppermute | solution.py:281
  47.5 11.4 %collective-permute-start.7 = (bf16[512,128]{1,0:T(8,128)(2,1)S(1)}, bf16[512,128]{1,0:T(8,128)(2,1)S(1)}, u32[]{:S(2)}, u32[]{:S(2)}) collective-permute-start(bf16[512,128]{1,0:T(8,128)(2,1)S(1)} %get-tuple-element.32), channel_id=1, source_target_pairs={{0,0},{4,1},{8,2},{12,3},{1,4},{5,5},{9,6},{13,7},{2,8},{6,9},{10,... | collective-permute-start | bytes 393224 | tf_op jit(solution)/shard_map/ppermute | solution.py:314
  48.2 18.1 %collective-permute-start.8 = (bf16[512,128]{1,0:T(8,128)(2,1)S(1)}, bf16[512,128]{1,0:T(8,128)(2,1)S(1)}, u32[]{:S(2)}, u32[]{:S(2)}) collective-permute-start(bf16[512,128]{1,0:T(8,128)(2,1)S(1)} %get-tuple-element.33), channel_id=1, source_target_pairs={{1,0},{5,1},{9,2},{13,3},{2,4},{6,5},{10,6},{14,7},{3,8},{7,9},{11... | collective-permute-start | bytes 393224 | tf_op jit(solution)/shard_map/ppermute | solution.py:314
  56.1 10.2 %collective-permute-start.9 = (bf16[512,128]{1,0:T(8,128)(2,1)S(1)}, bf16[512,128]{1,0:T(8,128)(2,1)S(1)}, u32[]{:S(2)}, u32[]{:S(2)}) collective-permute-start(bf16[512,128]{1,0:T(8,128)(2,1)S(1)} %get-tuple-element.34), channel_id=1, source_target_pairs={{2,0},{6,1},{10,2},{14,3},{3,4},{7,5},{11,6},{15,7},{0,8},{4,9},{8... | collective-permute-start | bytes 393224 | tf_op jit(solution)/shard_map/ppermute | solution.py:314
  56.1 10.2 %collective-permute-start.10 = (bf16[512,128]{1,0:T(8,128)(2,1)S(1)}, bf16[512,128]{1,0:T(8,128)(2,1)S(1)}, u32[]{:S(2)}, u32[]{:S(2)}) collective-permute-start(bf16[512,128]{1,0:T(8,128)(2,1)S(1)} %get-tuple-element.35), channel_id=1, source_target_pairs={{3,0},{7,1},{11,2},{15,3},{0,4},{4,5},{8,6},{12,7},{1,8},{5,9},{9,... | collective-permute-start | bytes 393224 | tf_op jit(solution)/shard_map/ppermute | solution.py:314
  58.9 8.4 %collective-permute-start.11 = (bf16[512,128]{1,0:T(8,128)(2,1)S(1)}, bf16[512,128]{1,0:T(8,128)(2,1)S(1)}, u32[]{:S(2)}, u32[]{:S(2)}) collective-permute-start(bf16[512,128]{1,0:T(8,128)(2,1)S(1)} %get-tuple-element.39), channel_id=1, source_target_pairs={{1,0},{2,1},{3,2},{0,3},{5,4},{6,5},{7,6},{4,7},{9,8},{10,9},{11,1... | collective-permute-start | bytes 393224 | tf_op jit(solution)/shard_map/ppermute | solution.py:315
  58.9 11.1 %collective-permute-start.12 = (bf16[512,128]{1,0:T(8,128)(2,1)S(1)}, bf16[512,128]{1,0:T(8,128)(2,1)S(1)}, u32[]{:S(2)}, u32[]{:S(2)}) collective-permute-start(bf16[512,128]{1,0:T(8,128)(2,1)S(1)} %get-tuple-element.40), channel_id=1, source_target_pairs={{2,0},{3,1},{0,2},{1,3},{6,4},{7,5},{4,6},{5,7},{10,8},{11,9},{8,1... | collective-permute-start | bytes 393224 | tf_op jit(solution)/shard_map/ppermute | solution.py:315
  66.3 4.4 %collective-permute-start.13 = (bf16[512,128]{1,0:T(8,128)(2,1)S(1)}, bf16[512,128]{1,0:T(8,128)(2,1)S(1)}, u32[]{:S(2)}, u32[]{:S(2)}) collective-permute-start(bf16[512,128]{1,0:T(8,128)(2,1)S(1)} %get-tuple-element.41), channel_id=1, source_target_pairs={{3,0},{0,1},{1,2},{2,3},{7,4},{4,5},{5,6},{6,7},{11,8},{8,9},{9,10... | collective-permute-start | bytes 393224 | tf_op jit(solution)/shard_map/ppermute | solution.py:315
